TPU v7x, 32 devices: a whole 2x2x4 slice. The times are simulated.
32 devices in a mesh: tm: 4 (over y, core), space: 8 (over z, x).
Axes of the slice: x: 2, y: 2, z: 4, core: 2. Of those that a mesh axis runs over, the one named last changes fastest.
Arguments:
- initial: float32 [24, 192, 256], P('space'), may hold values from -1 to 1
- coarse_guess: float32 [4, 24, 192, 256], P('tm', 'space'), may hold values from -1 to 1
- react_rate: float32 [24, 192, 256], P('space'), may hold values from 0.5 to 3
Outputs:
- corrected: float32 [4, 24, 192, 256], P('tm', 'space')
- defect: float32 [4, 24, 192, 256], P('tm', 'space')
All inputs are finite; a program needn't handle non-finite values.
Results may differ from a plain program's by a relative error of at most 0.00002.
Values sent between devices are 32-bit elements; how exact they have to be, the bound alone decides.
A program may use at most 64 MiB of HBM per device.

v0:
```python
import functools

import jax
import jax.numpy as jnp
from jax import lax
from jax.experimental import pallas as pl
from jax.experimental.pallas import tpu as pltpu
from jax.sharding import PartitionSpec as P

STEPS = 3
SUBLANES = 8

fine_diffuse = 0.04
fine_growth = 0.05
coarse_ratio = 4.0

MESH = pl.DeviceIdType.MESH

PIECES = 4


def slots(planes):
    kinds = dict(
        start=2 + PIECES, start_edge=1 + PIECES, rate=1, rate_edge=2, rate_core=3, again=PIECES, again_edge=2 * PIECES,
        chain=2 * planes, chain_edge=2, defect=1, corrected=planes,
    )
    first, total = {}, 0
    for kind, number in kinds.items():
        first[kind] = total
        total += number
    return first, total


def kernel(
    nt, ns, planes, half, wide, slot_of,
    initial, guess, rate_in, corrected_out, defect_out,
    start, rate, again, before, first, second, relaxed, coarse, offset, defect, after, reach,
    send, recv, local,
):
    tm, space = lax.axis_index("tm"), lax.axis_index("space")
    pair, side = lax.div(space, 2), lax.rem(space, 2)
    pairs = ns // 2
    mate = space + 1 - 2 * side
    block = 2 * planes
    length = block + 2 * STEPS
    rows = half + 2 * wide
    has_low, has_high = pair > 0, pair < pairs - 1
    has_next, has_previous = tm < nt - 1, tm > 0
    own = pl.ds(STEPS, block)

    for ref in (start, rate, again, before):
        zero_plane = jnp.zeros((STEPS,) + ref.shape[1:], jnp.float32)
        zero_rows = jnp.zeros((block, wide, ref.shape[2]), jnp.float32)
        ref[0:STEPS] = zero_plane
        ref[STEPS + block : length] = zero_plane
        ref[STEPS : STEPS + block, 0:wide] = zero_rows
        ref[STEPS : STEPS + block, wide + half : rows] = zero_rows

    barrier = pltpu.get_barrier_semaphore()
    count = jnp.int32(0)
    for step in (-1, 0, 1):
        for place in ("own", "mate", "low", "high"):
            if step == 0 and place == "own":
                continue
            there = {"own": space, "mate": mate, "low": space - 2, "high": space + 2}[place]
            tests = []
            if step:
                tests.append(has_next if step > 0 else has_previous)
            if place in ("low", "high"):
                tests.append(has_low if place == "low" else has_high)
            target = {"tm": tm + step, "space": there}
            if tests:
                valid = functools.reduce(jnp.logical_and, tests)

                @pl.when(valid)
                def _(target=target):
                    pl.semaphore_signal(barrier, inc=1, device_id=target, device_id_type=MESH)

                count = count + valid.astype(jnp.int32)
            else:
                pl.semaphore_signal(barrier, inc=1, device_id=target, device_id_type=MESH)
                count = count + 1
    for here, there in ((tm == 0, nt - 1), (tm == nt - 1, 0)):

        @pl.when(here)
        def _(there=there):
            pl.semaphore_signal(
                barrier, inc=1, device_id={"tm": there, "space": mate}, device_id_type=MESH
            )

        count = count + here.astype(jnp.int32)
    pl.semaphore_wait(barrier, count)

    def remote(src, dst, slot, to_tm, to_space):
        return pltpu.make_async_remote_copy(
            src_ref=src,
            dst_ref=dst,
            send_sem=send.at[slot],
            recv_sem=recv.at[slot],
            device_id={"tm": to_tm, "space": to_space},
            device_id_type=MESH,
        )

    def cut(ref, target):
        return ref.at[:, pl.ds(pl.multiple_of(target * (half - wide), SUBLANES), half + wide), :]

    def spot(ref, target, begin, size):
        at = pl.multiple_of(wide * (1 - target), SUBLANES)
        return ref.at[pl.ds(begin, size), pl.ds(at, half + wide), :]

    slab = STEPS + planes * side
    other = STEPS + planes * (1 - side)

    core = lax.rem(tm, 2)
    twin = tm + 1 - 2 * core
    lanes = start.shape[2] // 2

    def lane_half(ref, which):
        return ref.at[:, :, pl.ds(pl.multiple_of(which * lanes, lanes), lanes)]

    groups = (half + wide) // SUBLANES
    bounds = [groups * piece // PIECES * SUBLANES for piece in range(PIECES + 1)]

    def piece_of(ref, begin, size, piece, target=side):
        at = pl.multiple_of(wide * (1 - target) + bounds[piece], SUBLANES)
        return ref.at[pl.ds(begin, size), pl.ds(at, bounds[piece + 1] - bounds[piece]), :]

    def cut_piece(ref, target, piece):
        at = pl.multiple_of(target * (half - wide) + bounds[piece], SUBLANES)
        return ref.at[:, pl.ds(at, bounds[piece + 1] - bounds[piece]), :]

    rate_own = pltpu.make_async_copy(cut(rate_in, side), spot(rate, side, slab, planes), local.at[0])
    rate_mate = remote(
        lane_half(cut(rate_in, 1 - side), core),
        lane_half(spot(rate, 1 - side, slab, planes), core),
        slot_of["rate"],
        tm,
        mate,
    )
    initial_own = pltpu.make_async_copy(cut(initial, side), spot(start, side, slab, planes), local.at[1])
    guess_own = remote(
        cut(guess, side), spot(start, side, slab, planes), slot_of["start"], tm + 1, space
    )

    def to_mate(ref, to_tm):
        return [
            remote(
                cut_piece(ref, 1 - side, piece),
                piece_of(start, slab, planes, piece, 1 - side),
                slot_of["start"] + 1 + piece,
                to_tm,
                mate,
            )
            for piece in range(PIECES)
        ]

    guess_mate = to_mate(guess, tm + 1)
    initial_mate = to_mate(initial, 0)
    is_last = tm == nt - 1

    rate_mate.start()
    rate_own.start()

    @pl.when(has_next)
    def _():
        guess_own.start()
        for copy in guess_mate:
            copy.start()

    @pl.when(is_last)
    def _():
        for copy in initial_mate:
            copy.start()

    @pl.when(tm == 0)
    def _():
        initial_own.start()

    for ref in (first, second):
        @pl.when(jnp.logical_not(has_low))
        def _(ref=ref):
            ref[0:STEPS] = jnp.zeros((STEPS,) + ref.shape[1:], jnp.float32)

        @pl.when(jnp.logical_not(has_high))
        def _(ref=ref):
            ref[STEPS + block : length] = jnp.zeros((STEPS,) + ref.shape[1:], jnp.float32)

    row = lax.broadcasted_iota(jnp.int32, reach.shape, 0)
    outside = jnp.logical_or(
        jnp.logical_and(side == 0, row < wide), jnp.logical_and(side == 1, row >= wide + half)
    )
    reach[...] = jnp.where(outside, 0.0, fine_diffuse)

    low_place, high_place = STEPS + block, 0

    def edge_pieces(piece):
        slot = slot_of["start_edge"] + 1 + piece
        low = remote(
            piece_of(start, STEPS, STEPS, piece), piece_of(start, low_place, STEPS, piece),
            slot, tm, space - 2,
        )
        high = remote(
            piece_of(start, block, STEPS, piece), piece_of(start, high_place, STEPS, piece),
            slot, tm, space + 2,
        )
        return low, high

    start_edges = [edge_pieces(piece) for piece in range(PIECES)]
    start_low = remote(
        spot(start, side, STEPS, STEPS), spot(start, side, low_place, STEPS),
        slot_of["start_edge"], tm, space - 2,
    )
    start_high = remote(
        spot(start, side, block, STEPS), spot(start, side, high_place, STEPS),
        slot_of["start_edge"], tm, space + 2,
    )
    reach_rate = STEPS - 1
    rate_low_spot = lane_half(spot(rate, side, low_place, reach_rate), core)
    rate_high_spot = lane_half(spot(rate, side, high_place + 1, reach_rate), core)
    rate_low = remote(
        lane_half(spot(rate, side, STEPS, reach_rate), core), rate_low_spot,
        slot_of["rate_edge"], tm, space - 2,
    )
    rate_high = remote(
        lane_half(spot(rate, side, STEPS + block - reach_rate, reach_rate), core), rate_high_spot,
        slot_of["rate_edge"] + 1, tm, space + 2,
    )
    rate_other_spot = lane_half(spot(rate, side, other, planes), core)
    twin_mate = remote(rate_other_spot, rate_other_spot, slot_of["rate_core"], twin, space)
    twin_low = remote(rate_low_spot, rate_low_spot, slot_of["rate_core"] + 1, twin, space)
    twin_high = remote(rate_high_spot, rate_high_spot, slot_of["rate_core"] + 2, twin, space)

    own_low = jnp.logical_and(side == 0, has_low)
    own_high = jnp.logical_and(side == 1, has_high)
    other_low = jnp.logical_and(side == 1, has_low)
    other_high = jnp.logical_and(side == 0, has_high)

    rate_own.wait()
    pl.when(own_low)(rate_low.start)
    pl.when(own_high)(rate_high.start)

    @pl.when(tm == 0)
    def _():
        initial_own.wait()

    @pl.when(has_previous)
    def _():
        guess_own.wait_recv()

    pl.when(own_low)(start_low.start)
    pl.when(own_high)(start_high.start)

    rate_mate.wait_recv()
    pl.when(other_low)(rate_low.start)
    pl.when(other_high)(rate_high.start)
    twin_mate.start()

    for piece in range(PIECES):
        guess_mate[piece].wait_recv()
        pl.when(other_low)(start_edges[piece][0].start)
        pl.when(other_high)(start_edges[piece][1].start)

    @pl.when(has_high)
    def _():
        rate_low.wait_recv()
        twin_low.start()

    @pl.when(has_low)
    def _():
        rate_high.wait_recv()
        twin_high.start()

    twin_mate.wait_recv()
    pl.when(has_high)(twin_low.wait_recv)
    pl.when(has_low)(twin_high.wait_recv)

    @pl.when(jnp.logical_and(side == 0, has_high))
    def _():
        start_low.wait_recv()

    @pl.when(jnp.logical_and(side == 1, has_low))
    def _():
        start_high.wait_recv()

    @pl.when(jnp.logical_and(side == 1, has_high))
    def _():
        for low, high in start_edges:
            low.wait_recv()

    @pl.when(jnp.logical_and(side == 0, has_low))
    def _():
        for low, high in start_edges:
            high.wait_recv()

    keep = pltpu.make_async_copy(start, again, local.at[1])

    @pl.when(tm == 0)
    def _():
        keep.start()

    width = start.shape[2]
    lane = lax.broadcasted_iota(jnp.int32, reach.shape, 1)

    def change(ref, z):
        middle = ref[z]
        beside = ref[z + 1] + ref[z - 1]
        beside = beside + pltpu.roll(middle, 1, 0) + pltpu.roll(middle, rows - 1, 0)
        beside = beside + jnp.where(lane == 0, 0.0, pltpu.roll(middle, 1, 1))
        beside = beside + jnp.where(lane == width - 1, 0.0, pltpu.roll(middle, width - 1, 1))
        growth = rate[z] * (fine_growth - fine_growth * (middle * middle))
        return middle, reach[...] * beside + middle * (growth - 6.0 * fine_diffuse)

    def span(step):
        low = jnp.where(has_low, step, max(step, STEPS))
        high = jnp.where(has_high, length - step, min(length - step, STEPS + block))
        return low, high

    def fine(src, dst, step):
        def plane(z, carry):
            middle, delta = change(src, z)
            dst[z] = middle + delta
            return carry

        lax.fori_loop(*span(step), plane, 0)

    fine(start, first, 1)
    fine(first, second, 2)
    fine(second, relaxed, 3)

    given, given_low, given_high = [], [], []
    for piece in range(PIECES):
        slot = slot_of["again_edge"] + 2 * piece
        given.append(
            remote(
                piece_of(relaxed, STEPS, block, piece),
                piece_of(again, STEPS, block, piece),
                slot_of["again"] + piece,
                tm + 1,
                space,
            )
        )
        given_low.append(
            remote(
                piece_of(again, STEPS, STEPS, piece),
                piece_of(again, STEPS + block, STEPS, piece),
                slot,
                tm,
                space - 2,
            )
        )
        given_high.append(
            remote(
                piece_of(again, block, STEPS, piece),
                piece_of(again, 0, STEPS, piece),
                slot + 1,
                tm,
                space + 2,
            )
        )

    @pl.when(has_next)
    def _():
        for piece in range(PIECES):
            given[piece].start()

    @pl.when(tm == 0)
    def _():
        keep.wait()

    @pl.when(has_previous)
    def _():
        for piece in range(PIECES):
            given[piece].wait_recv()
            pl.when(has_low)(given_low[piece].start)
            pl.when(has_high)(given_high[piece].start)
        for piece in range(PIECES):
            pl.when(has_high)(given_low[piece].wait_recv)
            pl.when(has_low)(given_high[piece].wait_recv)

    def first_plane(z, carry):
        middle, delta = change(again, z)
        first[z] = middle + delta
        coarse[z] = middle + coarse_ratio * delta
        return carry

    lax.fori_loop(*span(1), first_plane, 0)
    fine(first, second, 2)

    order = []
    for depth in range(planes):
        order += [STEPS + depth, STEPS + block - 1 - depth]

    def row_span(z):
        at = pl.multiple_of(wide * (1 - side), SUBLANES)
        return (pl.ds(z, 1), pl.ds(at, half + wide), slice(None))

    passed = {
        z: remote(
            after.at[row_span(z)], before.at[row_span(z)], slot_of["chain"] + z - STEPS, tm + 1, space
        )
        for z in order
    }
    low_edge, high_edge = STEPS, STEPS + block - 1
    passed_low = remote(
        before.at[row_span(low_edge)], before.at[row_span(high_edge + 1)],
        slot_of["chain_edge"], tm, space - 2,
    )
    passed_high = remote(
        before.at[row_span(high_edge)], before.at[row_span(low_edge - 1)],
        slot_of["chain_edge"] + 1, tm, space + 2,
    )

    mine = pl.ds(pl.multiple_of(side * half, SUBLANES), half)
    middle_rows = pl.ds(wide, half)
    defect_stay = pltpu.make_async_copy(
        defect.at[pl.ds(slab, planes), middle_rows, :], defect_out.at[:, mine, :], local.at[2]
    )
    defect_go = remote(
        defect.at[pl.ds(other, planes), middle_rows, :], defect_out.at[:, mine, :],
        slot_of["defect"], tm, mate,
    )
    stay, go = {}, {}
    for z in order:
        place = (z - STEPS) % planes
        src = after.at[pl.ds(z, 1), middle_rows, :]
        dst = corrected_out.at[pl.ds(place, 1), mine, :]
        stay[z] = pltpu.make_async_copy(src, dst, local.at[3 + place])
        go[z] = remote(src, dst, slot_of["corrected"] + place, tm, mate)

    def at_home(z):
        return side == (z - STEPS) // planes

    def hand_in(z):
        pl.when(at_home(z))(stay[z].start)
        pl.when(jnp.logical_not(at_home(z)))(go[z].start)

    def last_plane(z):
        middle, delta = change(second, z)
        end = middle + delta
        defect[z] = end - relaxed[z]
        shift = end - coarse[z]
        offset[z] = shift
        after[z] = coarse[z] + shift

    def take_edges():
        passed[low_edge].wait_recv()
        pl.when(has_low)(passed_low.start)
        passed[high_edge].wait_recv()
        pl.when(has_high)(passed_high.start)

    pl.when(tm == 2)(take_edges)
    opens = jnp.logical_and(tm == 1, has_next)
    for index, z in enumerate(order):
        last_plane(z)
        if index:
            pl.when(opens)(passed[order[index - 1]].start)
    pl.when(opens)(passed[order[-1]].start)
    defect_go.start()
    defect_stay.start()

    later = tm > 1

    @pl.when(jnp.logical_not(later))
    def _():
        for z in order:
            hand_in(z)

    @pl.when(later)
    def _():
        pl.when(tm > 2)(take_edges)
        queue = order[2:]
        waiting = set(queue)

        def leave(z):
            pl.when(has_next)(passed[z].start)
            hand_in(z)

        for index, z in enumerate(order):
            while waiting & {z - 1, z, z + 1}:
                come = queue.pop(0)
                waiting.remove(come)
                passed[come].wait_recv()
            if z == low_edge:
                pl.when(has_low)(passed_high.wait_recv)
            if z == high_edge:
                pl.when(has_high)(passed_low.wait_recv)
            middle, delta = change(before, z)
            after[z] = middle + coarse_ratio * delta + offset[z]
            if index:
                leave(order[index - 1])
        leave(order[-1])
        pl.when(has_low)(passed_low.wait_send)
        pl.when(has_high)(passed_high.wait_send)

    onward = jnp.logical_and(tm > 0, has_next)

    @pl.when(is_last)
    def _():
        for copy in initial_mate:
            copy.wait_send()

    @pl.when(has_next)
    def _():
        guess_own.wait_send()
        for copy in guess_mate:
            copy.wait_send()

    rate_mate.wait_send()
    twin_mate.wait_send()
    pl.when(has_high)(twin_low.wait_send)
    pl.when(has_low)(twin_high.wait_send)
    pl.when(has_low)(rate_low.wait_send)
    pl.when(has_high)(rate_high.wait_send)
    pl.when(own_low)(start_low.wait_send)
    pl.when(own_high)(start_high.wait_send)

    @pl.when(other_low)
    def _():
        for low, high in start_edges:
            low.wait_send()

    @pl.when(other_high)
    def _():
        for low, high in start_edges:
            high.wait_send()

    @pl.when(has_next)
    def _():
        for piece in range(PIECES):
            given[piece].wait_send()

    @pl.when(has_previous)
    def _():
        for piece in range(PIECES):
            pl.when(has_low)(given_low[piece].wait_send)
            pl.when(has_high)(given_high[piece].wait_send)

    @pl.when(onward)
    def _():
        for z in order:
            passed[z].wait_send()

    defect_stay.wait()
    defect_go.wait()
    for z in order:
        pl.when(at_home(z))(stay[z].wait)
        pl.when(at_home(z))(go[z].wait_recv)
        pl.when(jnp.logical_not(at_home(z)))(go[z].wait_send)


def on_device(nt, ns, initial, coarse_guess, react_rate):
    planes, across, width = initial.shape
    half = across // 2
    wide = -(-(2 * STEPS + max(nt - 2, 0)) // SUBLANES) * SUBLANES
    length = 2 * planes + 2 * STEPS
    field = pltpu.VMEM((length, half + 2 * wide, width), jnp.float32)
    slot_of, total = slots(planes)
    shape = jax.ShapeDtypeStruct(initial.shape, jnp.float32)
    corrected, defect = pl.pallas_call(
        functools.partial(kernel, nt, ns, planes, half, wide, slot_of),
        out_shape=(shape, shape),
        in_specs=[pl.BlockSpec(memory_space=pl.ANY)] * 3,
        out_specs=[pl.BlockSpec(memory_space=pl.ANY)] * 2,
        scratch_shapes=[field] * 11
        + [
            pltpu.VMEM((half + 2 * wide, width), jnp.float32),
            pltpu.SemaphoreType.DMA((total,)),
            pltpu.SemaphoreType.DMA((total,)),
            pltpu.SemaphoreType.DMA((3 + planes,)),
        ],
        compiler_params=pltpu.CompilerParams(collective_id=0, has_side_effects=True),
    )(initial, coarse_guess[0], react_rate)
    return corrected[None], defect[None]


def solution(mesh):
    in_specs = (P("space", None, None), P("tm", "space", None, None), P("space", None, None))
    out_specs = (P("tm", "space", None, None), P("tm", "space", None, None))
    return jax.shard_map(
        functools.partial(on_device, mesh.shape["tm"], mesh.shape["space"]),
        mesh=mesh, in_specs=in_specs, out_specs=out_specs, check_vma=False,
    )
```

profile of v0, /device:TPU:13, one launch (start us, length us, event | category | flops | bytes accessed | tf_op | source)
XLA Modules:
  0.0 56.0 jit_solution(17644408517439981220)
XLA Ops:
  0.6 52.6 %shard_map.50 = (f32[3,192,256]{2,1,0:T(8,128)}, f32[3,192,256]{2,1,0:T(8,128)}) custom-call(f32[3,192,256]{2,1,0:T(8,128)} %initial.1, f32[3,192,256]{2,1,0:T(8,128)} %bitcast.3, f32[3,192,256]{2,1,0:T(8,128)} %rate_in.1), custom_call_target="tpu_custom_call" | custom-call | tf_op jit(solution)/shard_map/pallas_call | solution.py:559
  53.2 0.0 copy-start
  53.2 2.0 %copy.7 = f32[1,3,192,256]{3,2,1,0:T(8,128)} copy(f32[1,3,192,256]{3,2,1,0:T(8,128)} %bitcast.5) | data formatting | bytes 1179648
  55.2 0.0 copy-done
  55.2 0.8 %copy.8 = f32[1,3,192,256]{3,2,1,0:T(8,128)} copy(f32[1,3,192,256]{3,2,1,0:T(8,128)S(1)} %bitcast.4) | data formatting | bytes 1179648
Async XLA Ops:
  53.2 2.0 %copy-start = (f32[3,192,256]{2,1,0:T(8,128)S(1)}, f32[3,192,256]{2,1,0:T(8,128)}, u32[]{:S(2)}) copy-start(f32[3,192,256]{2,1,0:T(8,128)} %get-tuple-element.5) | copy-start | bytes 1769476
where the time goes:
time: 56.3 us; the launch traced here: 56 us
  Pallas kernels  52.6 us (93%)
  local copies, waits for them, and re-layouts  2.8 us (5%)
  between operations  0.65 us (1%)
    pallas_call x1, Pallas kernels, on_device(): pl.pallas_call(functools.partial(kernel, nt, ns, planes, half, wide, slot...  52.6 us
    unnamed x4, local copies, waits for them, and re-layouts  2.8 us

commit v1 on v0

--- a/solution.py
+++ b/solution.py
@@ -17,6 +17,7 @@
 MESH = pl.DeviceIdType.MESH
 
 PIECES = 4
+HALVES = 2
 
 
 def slots(planes):
@@ -548,8 +549,390 @@
         pl.when(jnp.logical_not(at_home(z)))(go[z].wait_send)
 
 
+def quarter_slots(nt):
+    kinds = dict(
+        start=nt * HALVES, rate=1, low_start=nt * HALVES, high_start=nt * HALVES, low_rate=1, high_rate=1,
+        low_again=nt, high_again=nt, low_first=1, high_first=1, low_offset=nt, high_offset=nt,
+        corrected=nt, defect=nt,
+    )
+    first, total = {}, 0
+    for kind, number in kinds.items():
+        first[kind] = total
+        total += number
+    return first, total
+
+
+def quarter_kernel(
+    nt, ns, planes, part, wide, recv_of, recv_total,
+    initial, guess, rate_in, corrected_out, defect_out,
+    start, again, rate, first, second, coarse, chain, offset, defect, reach,
+    send, recv,
+):
+    tm, space = lax.axis_index("tm"), lax.axis_index("space")
+    y, core = lax.div(tm, 2), lax.rem(tm, 2)
+    pair, x = lax.div(space, 2), lax.rem(space, 2)
+    levels, pairs = nt // 2, ns // 2
+    length = planes + 2 * STEPS
+    rows = part + 2 * wide
+    across, width = initial.shape[1], initial.shape[2]
+    low_own, high_own = STEPS, STEPS + planes
+    slab = 2 * pair + core
+    has_low, has_high = slab > 0, slab < ns - 1
+    quarter = 2 * y + x
+    low_to = {"tm": tm + 1 - 2 * core, "space": space - 2 * (1 - core)}
+    high_to = {"tm": tm + 1 - 2 * core, "space": space + 2 * core}
+
+    def window(which):
+        begin = jnp.clip(part * which - wide, 0, across - rows)
+        at = begin - part * which + 2 * wide
+        return pl.multiple_of(begin, SUBLANES), pl.multiple_of(at, SUBLANES)
+
+    my_begin, my_at = window(quarter)
+    body = pl.ds(wide, rows)
+    mine = pl.ds(2 * wide, part)
+
+    first_row, last_row = y + x == 0, quarter == nt - 1
+    edge_zero = jnp.zeros((length, wide, width), jnp.float32)
+    plane_zero = jnp.zeros((STEPS,) + start.shape[2:], jnp.float32)
+
+    def clear_rows(ref, k):
+        @pl.when(first_row)
+        def _():
+            ref[k, :, wide : 2 * wide] = edge_zero
+
+        @pl.when(last_row)
+        def _():
+            ref[k, :, 2 * wide + part : 3 * wide + part] = edge_zero
+
+    def clear_planes(ref, k):
+        @pl.when(jnp.logical_not(has_low))
+        def _():
+            ref[k, 0:low_own] = plane_zero
+
+        @pl.when(jnp.logical_not(has_high))
+        def _():
+            ref[k, high_own:length] = plane_zero
+
+    for k in range(nt):
+        clear_rows(start, k)
+        clear_planes(start, k)
+        clear_planes(again, k)
+        clear_planes(chain, k)
+    clear_rows(rate, 0)
+    clear_planes(rate, 0)
+    clear_planes(first, 0)
+    clear_planes(second, 0)
+
+    barrier = pltpu.get_barrier_semaphore()
+    for dy in range(levels):
+        for dx in range(2):
+            for dc in range(2):
+                if dy or dx or dc:
+                    there = {
+                        "tm": 2 * lax.rem(y + dy, levels) + lax.rem(core + dc, 2),
+                        "space": 2 * pair + lax.rem(x + dx, 2),
+                    }
+                    pl.semaphore_signal(barrier, inc=1, device_id=there, device_id_type=MESH)
+    count = jnp.int32(2 * nt - 1)
+    for far, there in (
+        (jnp.logical_and(core == 0, has_low), low_to),
+        (jnp.logical_and(core == 1, has_high), high_to),
+    ):
+
+        @pl.when(far)
+        def _(there=there):
+            pl.semaphore_signal(barrier, inc=1, device_id=there, device_id_type=MESH)
+
+        count = count + far.astype(jnp.int32)
+    pl.semaphore_wait(barrier, count)
+
+    sends = []
+    send_count = [0]
+
+    def remote(src, dst, slot, there, condition):
+        number = send_count[0]
+        send_count[0] += 1
+        copy = pltpu.make_async_remote_copy(
+            src_ref=src, dst_ref=dst, send_sem=send.at[number], recv_sem=recv.at[slot],
+            device_id=there, device_id_type=MESH,
+        )
+        sends.append((copy, condition))
+        return copy
+
+    def launch(src, dst, slot, there, condition):
+        copy = remote(src, dst, slot, there, condition)
+        pl.when(condition)(copy.start)
+
+    def arrive(dst, slot, condition=None):
+        copy = pltpu.make_async_copy(dst, dst, recv.at[slot])
+        if condition is None:
+            copy.wait()
+        else:
+            pl.when(condition)(copy.wait)
+
+    size = rows // HALVES
+    own = pl.ds(low_own, planes)
+    home = core == x
+    away = jnp.logical_not(home)
+
+    def source(ref, begin, half):
+        return ref.at[:, pl.ds(pl.multiple_of(begin + half * size, SUBLANES), size), :]
+
+    def place(ref, k, at, half, zs=own):
+        return ref.at[k, zs, pl.ds(pl.multiple_of(at + half * size, SUBLANES), size), :]
+
+    def whole(ref, k, at, zs=own):
+        return ref.at[k, zs, pl.ds(at, rows), :]
+
+    @pl.when(home)
+    def _():
+        pltpu.make_async_copy(
+            rate_in.at[:, pl.ds(my_begin, rows), :], whole(rate, 0, my_at), recv.at[recv_of["rate"]]
+        ).start()
+        for half in range(HALVES):
+            pltpu.make_async_copy(
+                source(initial, my_begin, half), place(start, 0, my_at, half), recv.at[recv_of["start"] + half]
+            ).start()
+
+    rate_level = tm - levels
+    gives_rate = rate_level >= 0
+    rate_begin, rate_at = window(2 * rate_level + 1 - x)
+    launch(
+        rate_in.at[:, pl.ds(rate_begin, rows), :], whole(rate, 0, rate_at), recv_of["rate"],
+        {"tm": 2 * rate_level + x, "space": space + 1 - 2 * x}, gives_rate,
+    )
+    there_begin, there_at = window(2 * y + 1 - x)
+    for half in range(HALVES):
+        launch(
+            source(initial, there_begin, half), place(start, 0, there_at, half), recv_of["start"] + half,
+            {"tm": 2 * y + x, "space": space + 1 - 2 * x}, core == half % 2,
+        )
+    gives_guess = tm < nt - 1
+    for half in range(HALVES):
+        slot = recv_of["start"] + (tm + 1) * HALVES + half
+        for dy in range(levels):
+            for dx in (1, 0):
+                to_y, to_x = lax.rem(y + dy, levels), lax.rem(x + dx, 2)
+                begin, at = window(2 * to_y + to_x)
+                src, dst = source(guess, begin, half), place(start, tm + 1, at, half)
+                there = {"tm": 2 * to_y + x, "space": 2 * pair + to_x}
+                if dy or dx:
+                    launch(src, dst, slot, there, gives_guess)
+                else:
+                    launch(src, dst, slot, there, jnp.logical_and(gives_guess, away))
+
+                    @pl.when(jnp.logical_and(gives_guess, home))
+                    def _(src=src, dst=dst, slot=slot):
+                        pltpu.make_async_copy(src, dst, recv.at[slot]).start()
+
+    row = lax.broadcasted_iota(jnp.int32, reach.shape, 0)
+    outside = jnp.logical_or(
+        jnp.logical_and(first_row, row < wide), jnp.logical_and(last_row, row >= wide + part)
+    )
+    reach[...] = jnp.where(outside, 0.0, fine_diffuse)
+    lane = lax.broadcasted_iota(jnp.int32, reach.shape, 1)
+
+    def share(src_of, depth, high_slot, low_slot):
+        launch(
+            src_of(pl.ds(low_own, depth)), src_of(pl.ds(high_own, depth)), high_slot, low_to, has_low
+        )
+        launch(
+            src_of(pl.ds(high_own - depth, depth)), src_of(pl.ds(low_own - depth, depth)), low_slot, high_to, has_high
+        )
+
+    def shared(dst_of, depth, high_slot, low_slot):
+        arrive(dst_of(pl.ds(high_own, depth)), high_slot, has_high)
+        arrive(dst_of(pl.ds(low_own - depth, depth)), low_slot, has_low)
+
+    def start_view(k, half):
+        return lambda zs: place(start, k, my_at, half, zs)
+
+    def relay_start(k, half):
+        at = k * HALVES + half
+        arrive(place(start, k, my_at, half), recv_of["start"] + at)
+        share(start_view(k, half), STEPS, recv_of["high_start"] + at, recv_of["low_start"] + at)
+
+    def start_ready(k):
+        for half in range(HALVES):
+            at = k * HALVES + half
+            shared(start_view(k, half), STEPS, recv_of["high_start"] + at, recv_of["low_start"] + at)
+
+    def rate_view(zs):
+        return whole(rate, 0, my_at, zs)
+
+    def body_view(ref, k):
+        return lambda zs: ref.at[k, zs, body, :]
+
+    def change(ref, k, z):
+        middle = ref[k, z, body, :]
+        beside = ref[k, z + 1, body, :] + ref[k, z - 1, body, :]
+        beside = beside + pltpu.roll(middle, 1, 0) + pltpu.roll(middle, rows - 1, 0)
+        beside = beside + jnp.where(lane == 0, 0.0, pltpu.roll(middle, 1, 1))
+        beside = beside + jnp.where(lane == width - 1, 0.0, pltpu.roll(middle, width - 1, 1))
+        growth = rate[0, z, body, :] * (fine_growth - fine_growth * (middle * middle))
+        return middle, reach[...] * beside + middle * (growth - 6.0 * fine_diffuse)
+
+    def span(halo):
+        low = jnp.where(has_low, low_own - halo, low_own)
+        high = jnp.where(has_high, high_own + halo, high_own)
+        return low, high
+
+    def fine(src, source_k, dst, dst_k, halo, rough=False):
+        def plane(z, carry):
+            middle, delta = change(src, source_k, z)
+            dst[dst_k, z, body, :] = middle + delta
+            if rough:
+                coarse[0, z, body, :] = middle + coarse_ratio * delta
+            return carry
+
+        lax.fori_loop(*span(halo), plane, 0)
+
+    def hand_in(ref, k, out, kind, j):
+        there_space = 2 * pair + core
+        src = ref.at[k, own, mine, :]
+        dst = out.at[:, pl.ds(pl.multiple_of(part * quarter, SUBLANES), part), :]
+        slot = recv_of[kind] + quarter
+        stays = jnp.logical_and(tm == j, home)
+        launch(src, dst, slot, {"tm": j, "space": there_space}, jnp.logical_not(stays))
+
+        @pl.when(stays)
+        def _():
+            pltpu.make_async_copy(src, dst, recv.at[slot]).start()
+
+    def relax(k):
+        fine(start, k, first, 0, 2, rough=k == 0)
+        fine(first, 0, second, 0, 1)
+        if k:
+            fine(second, 0, again, k, 0)
+            return
+
+        def plane(z, carry):
+            middle, delta = change(second, 0, z)
+            value = middle + delta
+            again[0, z, body, :] = value
+            defect[0, z, body, :] = value - value
+            base = coarse[0, z, body, :]
+            chain[0, z, body, :] = base + (value - base)
+            return carry
+
+        lax.fori_loop(low_own, high_own, plane, 0)
+
+    def send_again(k):
+        share(body_view(again, k), STEPS, recv_of["high_again"] + k, recv_of["low_again"] + k)
+
+    def finish(k):
+        shared(body_view(again, k), STEPS, recv_of["high_again"] + k, recv_of["low_again"] + k)
+        fine(again, k, first, 0, 2, rough=True)
+        fine(first, 0, second, 0, 1)
+
+        def plane(z, carry):
+            middle, delta = change(second, 0, z)
+            value = middle + delta
+            defect[k + 1, z, body, :] = value - again[k + 1, z, body, :]
+            base = coarse[0, z, body, :]
+            if k:
+                offset[k + 1, z, body, :] = value - base
+            else:
+                chain[1, z, body, :] = base + (value - base)
+            return carry
+
+        lax.fori_loop(low_own, high_own, plane, 0)
+
+    arrive(rate_view(own), recv_of["rate"])
+    share(rate_view, STEPS - 1, recv_of["high_rate"], recv_of["low_rate"])
+    for half in range(HALVES):
+        relay_start(0, half)
+    for half in range(HALVES):
+        for k in range(1, nt - 1):
+            relay_start(k, half)
+
+    shared(rate_view, STEPS - 1, recv_of["high_rate"], recv_of["low_rate"])
+    start_ready(0)
+    relax(0)
+    send_again(0)
+    hand_in(chain, 0, corrected_out, "corrected", 0)
+    hand_in(defect, 0, defect_out, "defect", 0)
+    for half in range(HALVES):
+        relay_start(nt - 1, half)
+    for k in range(1, nt - 1):
+        start_ready(k)
+        relax(k)
+        send_again(k)
+
+    reaches = nt - 2
+    finish(0)
+    share(body_view(chain, 1), reaches, recv_of["high_first"], recv_of["low_first"])
+    hand_in(chain, 1, corrected_out, "corrected", 1)
+    hand_in(defect, 1, defect_out, "defect", 1)
+    start_ready(nt - 1)
+    relax(nt - 1)
+    for k in range(1, nt - 1):
+        finish(k)
+        j = k + 1
+        if nt - 1 - j:
+            share(body_view(offset, j), nt - 1 - j, recv_of["high_offset"] + j, recv_of["low_offset"] + j)
+        hand_in(defect, j, defect_out, "defect", j)
+
+    shared(body_view(chain, 1), reaches, recv_of["high_first"], recv_of["low_first"])
+    for j in range(2, nt):
+        halo = nt - 1 - j
+        if halo:
+            shared(body_view(offset, j), halo, recv_of["high_offset"] + j, recv_of["low_offset"] + j)
+
+        def plane(z, carry, j=j):
+            middle, delta = change(chain, j - 1, z)
+            chain[j, z, body, :] = middle + coarse_ratio * delta + offset[j, z, body, :]
+            return carry
+
+        lax.fori_loop(*span(halo), plane, 0)
+        hand_in(chain, j, corrected_out, "corrected", j)
+
+    for copy, condition in sends:
+        pl.when(condition)(copy.wait_send)
+    for out, kind in ((corrected_out, "corrected"), (defect_out, "defect")):
+        for q in range(nt):
+            arrive(out.at[:, pl.ds(part * q, part), :], recv_of[kind] + q)
+
+
+def quarter_device(nt, ns, initial, coarse_guess, react_rate):
+    planes, across, width = initial.shape
+    part = across // nt
+    wide = -(-(2 * STEPS + max(nt - 2, 0)) // SUBLANES) * SUBLANES
+    length = planes + 2 * STEPS
+    tall = part + 4 * wide
+    recv_of, recv_total = quarter_slots(nt)
+
+    def field(number):
+        return pltpu.VMEM((number, length, tall, width), jnp.float32)
+
+    shape = jax.ShapeDtypeStruct(initial.shape, jnp.float32)
+    corrected, defect = pl.pallas_call(
+        functools.partial(quarter_kernel, nt, ns, planes, part, wide, recv_of, recv_total),
+        out_shape=(shape, shape),
+        in_specs=[pl.BlockSpec(memory_space=pl.ANY)] * 3,
+        out_specs=[pl.BlockSpec(memory_space=pl.ANY)] * 2,
+        scratch_shapes=[
+            field(nt), field(nt), field(1), field(1), field(1), field(1), field(nt), field(nt), field(nt),
+            pltpu.VMEM((part + 2 * wide, width), jnp.float32),
+            pltpu.SemaphoreType.DMA((200,)),
+            pltpu.SemaphoreType.DMA((recv_total,)),
+        ],
+        compiler_params=pltpu.CompilerParams(collective_id=0, has_side_effects=True),
+    )(initial, coarse_guess[0], react_rate)
+    return corrected[None], defect[None]
+
+
+def takes_quarters(nt, planes, across):
+    part = across // nt
+    wide = -(-(2 * STEPS + max(nt - 2, 0)) // SUBLANES) * SUBLANES
+    fits = across % (nt * SUBLANES) == 0 and part + 2 * wide <= across and nt - 2 <= planes
+    return nt % 2 == 0 and nt > 2 and planes >= STEPS and fits
+
+
 def on_device(nt, ns, initial, coarse_guess, react_rate):
     planes, across, width = initial.shape
+    if takes_quarters(nt, planes, across):
+        return quarter_device(nt, ns, initial, coarse_guess, react_rate)
     half = across // 2
     wide = -(-(2 * STEPS + max(nt - 2, 0)) // SUBLANES) * SUBLANES
     length = 2 * planes + 2 * STEPS

time: 56.3 us -> 46.7 us (0.83)
  Pallas kernels: 52.6 us -> 43.1 us
    pallas_call x1, Pallas kernels: 52.6 us -> 43.1 us  [quarter_device(): pl.pallas_call(functools.partial(quarter_kernel, nt, ns, planes, part, wi...]
where the time goes in v1:
time: 46.7 us; the launch traced here: 46.6 us
  Pallas kernels  43.1 us (92%)
  local copies, waits for them, and re-layouts  2.8 us (6%)
  between operations  0.65 us (1%)
    pallas_call x1, Pallas kernels, quarter_device(): pl.pallas_call(functools.partial(quarter_kernel, nt, ns, planes, part, wi...  43.1 us
    unnamed x4, local copies, waits for them, and re-layouts  2.8 us

profile of v1, /device:TPU:13, one launch (start us, length us, event | category | flops | bytes accessed | tf_op | source)
XLA Modules:
  0.0 46.6 jit_solution(2492497902143598741)
XLA Ops:
  0.6 43.1 %shard_map.50 = (f32[3,192,256]{2,1,0:T(8,128)}, f32[3,192,256]{2,1,0:T(8,128)}) custom-call(f32[3,192,256]{2,1,0:T(8,128)} %initial.1, f32[3,192,256]{2,1,0:T(8,128)} %bitcast.3, f32[3,192,256]{2,1,0:T(8,128)} %rate_in.1), custom_call_target="tpu_custom_call" | custom-call | tf_op jit(solution)/shard_map/pallas_call | solution.py:909
  43.8 0.0 copy-start
  43.8 2.0 %copy.7 = f32[1,3,192,256]{3,2,1,0:T(8,128)} copy(f32[1,3,192,256]{3,2,1,0:T(8,128)} %bitcast.5) | data formatting | bytes 1179648
  45.8 0.0 copy-done
  45.8 0.8 %copy.8 = f32[1,3,192,256]{3,2,1,0:T(8,128)} copy(f32[1,3,192,256]{3,2,1,0:T(8,128)S(1)} %bitcast.4) | data formatting | bytes 1179648
Async XLA Ops:
  43.8 2.0 %copy-start = (f32[3,192,256]{2,1,0:T(8,128)S(1)}, f32[3,192,256]{2,1,0:T(8,128)}, u32[]{:S(2)}) copy-start(f32[3,192,256]{2,1,0:T(8,128)} %get-tuple-element.5) | copy-start | bytes 1769476

commit v2 on v1

--- a/solution.py
+++ b/solution.py
@@ -17,7 +17,8 @@
 MESH = pl.DeviceIdType.MESH
 
 PIECES = 4
-HALVES = 2
+SHARES = 4
+VMEM_BYTES = 40 << 20
 
 
 def slots(planes):
@@ -551,7 +552,8 @@
 
 def quarter_slots(nt):
     kinds = dict(
-        start=nt * HALVES, rate=1, low_start=nt * HALVES, high_start=nt * HALVES, low_rate=1, high_rate=1,
+        start=nt * SHARES, rate=SHARES, low_start=nt * SHARES, high_start=nt * SHARES,
+        low_rate=SHARES, high_rate=SHARES,
         low_again=nt, high_again=nt, low_first=1, high_first=1, low_offset=nt, high_offset=nt,
         corrected=nt, defect=nt,
     )
@@ -565,7 +567,7 @@
 def quarter_kernel(
     nt, ns, planes, part, wide, recv_of, recv_total,
     initial, guess, rate_in, corrected_out, defect_out,
-    start, again, rate, first, second, coarse, chain, offset, defect, reach,
+    start, again, rate, first, second, coarse, chain, offset, defect, end, reach,
     send, recv,
 ):
     tm, space = lax.axis_index("tm"), lax.axis_index("space")
@@ -613,16 +615,6 @@
         def _():
             ref[k, high_own:length] = plane_zero
 
-    for k in range(nt):
-        clear_rows(start, k)
-        clear_planes(start, k)
-        clear_planes(again, k)
-        clear_planes(chain, k)
-    clear_rows(rate, 0)
-    clear_planes(rate, 0)
-    clear_planes(first, 0)
-    clear_planes(second, 0)
-
     barrier = pltpu.get_barrier_semaphore()
     for dy in range(levels):
         for dx in range(2):
@@ -644,6 +636,17 @@
             pl.semaphore_signal(barrier, inc=1, device_id=there, device_id_type=MESH)
 
         count = count + far.astype(jnp.int32)
+
+    for k in range(nt):
+        clear_rows(start, k)
+        clear_planes(start, k)
+        clear_planes(again, k)
+        clear_planes(chain, k)
+    clear_rows(rate, 0)
+    clear_planes(rate, 0)
+    clear_planes(first, 0)
+    clear_planes(second, 0)
+
     pl.semaphore_wait(barrier, count)
 
     sends = []
@@ -670,60 +673,60 @@
         else:
             pl.when(condition)(copy.wait)
 
-    size = rows // HALVES
+    size = rows // SHARES
     own = pl.ds(low_own, planes)
     home = core == x
     away = jnp.logical_not(home)
 
-    def source(ref, begin, half):
-        return ref.at[:, pl.ds(pl.multiple_of(begin + half * size, SUBLANES), size), :]
-
-    def place(ref, k, at, half, zs=own):
-        return ref.at[k, zs, pl.ds(pl.multiple_of(at + half * size, SUBLANES), size), :]
-
-    def whole(ref, k, at, zs=own):
-        return ref.at[k, zs, pl.ds(at, rows), :]
+    def source(ref, begin, share_at):
+        return ref.at[:, pl.ds(pl.multiple_of(begin + share_at * size, SUBLANES), size), :]
+
+    def place(ref, k, at, share_at, zs=own):
+        return ref.at[k, zs, pl.ds(pl.multiple_of(at + share_at * size, SUBLANES), size), :]
 
     @pl.when(home)
     def _():
-        pltpu.make_async_copy(
-            rate_in.at[:, pl.ds(my_begin, rows), :], whole(rate, 0, my_at), recv.at[recv_of["rate"]]
-        ).start()
-        for half in range(HALVES):
-            pltpu.make_async_copy(
-                source(initial, my_begin, half), place(start, 0, my_at, half), recv.at[recv_of["start"] + half]
-            ).start()
-
-    rate_level = tm - levels
-    gives_rate = rate_level >= 0
-    rate_begin, rate_at = window(2 * rate_level + 1 - x)
-    launch(
-        rate_in.at[:, pl.ds(rate_begin, rows), :], whole(rate, 0, rate_at), recv_of["rate"],
-        {"tm": 2 * rate_level + x, "space": space + 1 - 2 * x}, gives_rate,
-    )
+        for ref, k, src, kind in ((start, 0, initial, "start"), (rate, 0, rate_in, "rate")):
+            for share_at in range(SHARES):
+                pltpu.make_async_copy(
+                    source(src, my_begin, share_at), place(ref, k, my_at, share_at), recv.at[recv_of[kind] + share_at]
+                ).start()
+
     there_begin, there_at = window(2 * y + 1 - x)
-    for half in range(HALVES):
+    for share_at in range(SHARES):
         launch(
-            source(initial, there_begin, half), place(start, 0, there_at, half), recv_of["start"] + half,
-            {"tm": 2 * y + x, "space": space + 1 - 2 * x}, core == half % 2,
+            source(initial, there_begin, share_at), place(start, 0, there_at, share_at),
+            recv_of["start"] + share_at, {"tm": 2 * y + x, "space": space + 1 - 2 * x}, core == share_at % 2,
         )
-    gives_guess = tm < nt - 1
-    for half in range(HALVES):
-        slot = recv_of["start"] + (tm + 1) * HALVES + half
-        for dy in range(levels):
-            for dx in (1, 0):
-                to_y, to_x = lax.rem(y + dy, levels), lax.rem(x + dx, 2)
-                begin, at = window(2 * to_y + to_x)
-                src, dst = source(guess, begin, half), place(start, tm + 1, at, half)
-                there = {"tm": 2 * to_y + x, "space": 2 * pair + to_x}
-                if dy or dx:
-                    launch(src, dst, slot, there, gives_guess)
-                else:
-                    launch(src, dst, slot, there, jnp.logical_and(gives_guess, away))
-
-                    @pl.when(jnp.logical_and(gives_guess, home))
-                    def _(src=src, dst=dst, slot=slot):
-                        pltpu.make_async_copy(src, dst, recv.at[slot]).start()
+    for to_y in range(levels):
+        begin, at = window(2 * to_y + 1 - x)
+        for share_at in range(SHARES):
+            launch(
+                source(rate_in, begin, share_at), place(rate, 0, at, share_at), recv_of["rate"] + share_at,
+                {"tm": 2 * to_y + x, "space": space + 1 - 2 * x},
+                jnp.logical_and(y == levels - 1, core == share_at % 2),
+            )
+
+    def give_guess(turn):
+        gives = jnp.logical_and(tm < nt - 1, core == turn)
+        for share_at in range(SHARES):
+            slot = recv_of["start"] + (tm + 1) * SHARES + share_at
+            for dy in range(levels):
+                for dx in (1, 0):
+                    to_y, to_x = lax.rem(y + dy, levels), lax.rem(x + dx, 2)
+                    begin, at = window(2 * to_y + to_x)
+                    src, dst = source(guess, begin, share_at), place(start, tm + 1, at, share_at)
+                    there = {"tm": 2 * to_y + x, "space": 2 * pair + to_x}
+                    if dy or dx:
+                        launch(src, dst, slot, there, gives)
+                    else:
+                        launch(src, dst, slot, there, jnp.logical_and(gives, away))
+
+                        @pl.when(jnp.logical_and(gives, home))
+                        def _(src=src, dst=dst, slot=slot):
+                            pltpu.make_async_copy(src, dst, recv.at[slot]).start()
+
+    give_guess(0)
 
     row = lax.broadcasted_iota(jnp.int32, reach.shape, 0)
     outside = jnp.logical_or(
@@ -744,21 +747,31 @@
         arrive(dst_of(pl.ds(high_own, depth)), high_slot, has_high)
         arrive(dst_of(pl.ds(low_own - depth, depth)), low_slot, has_low)
 
-    def start_view(k, half):
-        return lambda zs: place(start, k, my_at, half, zs)
-
-    def relay_start(k, half):
-        at = k * HALVES + half
-        arrive(place(start, k, my_at, half), recv_of["start"] + at)
-        share(start_view(k, half), STEPS, recv_of["high_start"] + at, recv_of["low_start"] + at)
+    def start_view(k, share_at):
+        return lambda zs: place(start, k, my_at, share_at, zs)
+
+    def relay_start(k):
+        for share_at in range(SHARES):
+            at = k * SHARES + share_at
+            arrive(place(start, k, my_at, share_at), recv_of["start"] + at)
+            share(start_view(k, share_at), STEPS, recv_of["high_start"] + at, recv_of["low_start"] + at)
 
     def start_ready(k):
-        for half in range(HALVES):
-            at = k * HALVES + half
-            shared(start_view(k, half), STEPS, recv_of["high_start"] + at, recv_of["low_start"] + at)
-
-    def rate_view(zs):
-        return whole(rate, 0, my_at, zs)
+        for share_at in range(SHARES):
+            at = k * SHARES + share_at
+            shared(start_view(k, share_at), STEPS, recv_of["high_start"] + at, recv_of["low_start"] + at)
+
+    def rate_view(share_at):
+        return lambda zs: place(rate, 0, my_at, share_at, zs)
+
+    def relay_rate():
+        for at in range(SHARES):
+            arrive(place(rate, 0, my_at, at), recv_of["rate"] + at)
+            share(rate_view(at), STEPS - 1, recv_of["high_rate"] + at, recv_of["low_rate"] + at)
+
+    def rate_ready():
+        for at in range(SHARES):
+            shared(rate_view(at), STEPS - 1, recv_of["high_rate"] + at, recv_of["low_rate"] + at)
 
     def body_view(ref, k):
         return lambda zs: ref.at[k, zs, body, :]
@@ -802,17 +815,18 @@
     def relax(k):
         fine(start, k, first, 0, 2, rough=k == 0)
         fine(first, 0, second, 0, 1)
-        if k:
-            fine(second, 0, again, k, 0)
-            return
 
         def plane(z, carry):
             middle, delta = change(second, 0, z)
             value = middle + delta
-            again[0, z, body, :] = value
-            defect[0, z, body, :] = value - value
-            base = coarse[0, z, body, :]
-            chain[0, z, body, :] = base + (value - base)
+            if k == nt - 1:
+                defect[k, z, body, :] = end[0, z, body, :] - value
+                return carry
+            again[k, z, body, :] = value
+            if k == 0:
+                defect[0, z, body, :] = value - value
+                base = coarse[0, z, body, :]
+                chain[0, z, body, :] = base + (value - base)
             return carry
 
         lax.fori_loop(low_own, high_own, plane, 0)
@@ -828,7 +842,10 @@
         def plane(z, carry):
             middle, delta = change(second, 0, z)
             value = middle + delta
-            defect[k + 1, z, body, :] = value - again[k + 1, z, body, :]
+            if k + 1 < nt - 1:
+                defect[k + 1, z, body, :] = value - again[k + 1, z, body, :]
+            else:
+                end[0, z, body, :] = value
             base = coarse[0, z, body, :]
             if k:
                 offset[k + 1, z, body, :] = value - base
@@ -838,60 +855,93 @@
 
         lax.fori_loop(low_own, high_own, plane, 0)
 
-    arrive(rate_view(own), recv_of["rate"])
-    share(rate_view, STEPS - 1, recv_of["high_rate"], recv_of["low_rate"])
-    for half in range(HALVES):
-        relay_start(0, half)
-    for half in range(HALVES):
-        for k in range(1, nt - 1):
-            relay_start(k, half)
-
-    shared(rate_view, STEPS - 1, recv_of["high_rate"], recv_of["low_rate"])
+    def lift_between(j, low, high):
+        def plane(z, carry):
+            middle, delta = change(chain, j - 1, z)
+            chain[j, z, body, :] = middle + coarse_ratio * delta + offset[j, z, body, :]
+            return carry
+
+        lax.fori_loop(low, high, plane, 0)
+
+    def edges_of(j):
+        slots = recv_of["high_offset"] + j, recv_of["low_offset"] + j
+        return body_view(offset, j), nt - 1 - j, *slots
+
+    def lift_around(j):
+        if nt - 1 - j:
+            shared(*edges_of(j))
+            low, high = span(nt - 1 - j)
+            lift_between(j, low, low_own)
+            lift_between(j, high_own, high)
+
+    relay_start(0)
+    relay_rate()
+    give_guess(1)
+    relay_start(1)
     start_ready(0)
+    rate_ready()
     relax(0)
     send_again(0)
     hand_in(chain, 0, corrected_out, "corrected", 0)
     hand_in(defect, 0, defect_out, "defect", 0)
-    for half in range(HALVES):
-        relay_start(nt - 1, half)
-    for k in range(1, nt - 1):
-        start_ready(k)
-        relax(k)
-        send_again(k)
-
-    reaches = nt - 2
+    relay_start(2)
+    start_ready(1)
+    relax(1)
+    send_again(1)
     finish(0)
-    share(body_view(chain, 1), reaches, recv_of["high_first"], recv_of["low_first"])
+    first_edges = body_view(chain, 1), nt - 2, recv_of["high_first"], recv_of["low_first"]
+    share(*first_edges)
     hand_in(chain, 1, corrected_out, "corrected", 1)
     hand_in(defect, 1, defect_out, "defect", 1)
+    for j in range(2, nt):
+        if j < nt - 1:
+            start_ready(j)
+            relax(j)
+            send_again(j)
+        if j + 1 < nt:
+            relay_start(j + 1)
+        finish(j - 1)
+        if j < nt - 1:
+            hand_in(defect, j, defect_out, "defect", j)
+            share(*edges_of(j))
+        if j == 2:
+            shared(*first_edges)
+        else:
+            lift_around(j - 1)
+        lift_between(j, low_own, high_own)
+        hand_in(chain, j, corrected_out, "corrected", j)
     start_ready(nt - 1)
     relax(nt - 1)
-    for k in range(1, nt - 1):
-        finish(k)
-        j = k + 1
-        if nt - 1 - j:
-            share(body_view(offset, j), nt - 1 - j, recv_of["high_offset"] + j, recv_of["low_offset"] + j)
-        hand_in(defect, j, defect_out, "defect", j)
-
-    shared(body_view(chain, 1), reaches, recv_of["high_first"], recv_of["low_first"])
-    for j in range(2, nt):
-        halo = nt - 1 - j
-        if halo:
-            shared(body_view(offset, j), halo, recv_of["high_offset"] + j, recv_of["low_offset"] + j)
-
-        def plane(z, carry, j=j):
-            middle, delta = change(chain, j - 1, z)
-            chain[j, z, body, :] = middle + coarse_ratio * delta + offset[j, z, body, :]
-            return carry
-
-        lax.fori_loop(*span(halo), plane, 0)
-        hand_in(chain, j, corrected_out, "corrected", j)
+    hand_in(defect, nt - 1, defect_out, "defect", nt - 1)
 
     for copy, condition in sends:
         pl.when(condition)(copy.wait_send)
     for out, kind in ((corrected_out, "corrected"), (defect_out, "defect")):
         for q in range(nt):
             arrive(out.at[:, pl.ds(part * q, part), :], recv_of[kind] + q)
+
+
+def settle_kernel(corrected, defect, corrected_out, defect_out, local):
+    copies = (
+        pltpu.make_async_copy(corrected, corrected_out.at[0], local.at[0]),
+        pltpu.make_async_copy(defect, defect_out.at[0], local.at[1]),
+    )
+    for copy in copies:
+        copy.start()
+    for copy in copies:
+        copy.wait()
+
+
+def settle(corrected, defect):
+    shape = jax.ShapeDtypeStruct((1,) + corrected.shape, jnp.float32)
+    return pl.pallas_call(
+        settle_kernel,
+        out_shape=(shape, shape),
+        in_specs=[pl.BlockSpec(memory_space=pl.ANY)] * 2,
+        out_specs=[pl.BlockSpec(memory_space=pl.ANY)] * 2,
+        scratch_shapes=[pltpu.SemaphoreType.DMA((2,))],
+        compiler_params=pltpu.CompilerParams(vmem_limit_bytes=1 << 20),
+    )(corrected, defect)
 
 
 def quarter_device(nt, ns, initial, coarse_guess, react_rate):
@@ -909,17 +959,17 @@
     corrected, defect = pl.pallas_call(
         functools.partial(quarter_kernel, nt, ns, planes, part, wide, recv_of, recv_total),
         out_shape=(shape, shape),
-        in_specs=[pl.BlockSpec(memory_space=pl.ANY)] * 3,
+        in_specs=[pl.BlockSpec(memory_space=pltpu.HBM)] * 3,
         out_specs=[pl.BlockSpec(memory_space=pl.ANY)] * 2,
         scratch_shapes=[
-            field(nt), field(nt), field(1), field(1), field(1), field(1), field(nt), field(nt), field(nt),
+            field(nt), field(nt), field(1), field(1), field(1), field(1), field(nt), field(nt), field(nt), field(1),
             pltpu.VMEM((part + 2 * wide, width), jnp.float32),
-            pltpu.SemaphoreType.DMA((200,)),
+            pltpu.SemaphoreType.DMA((SHARES * (4 * nt + nt // 2 + 3) + 6 * nt - 6,)),
             pltpu.SemaphoreType.DMA((recv_total,)),
         ],
-        compiler_params=pltpu.CompilerParams(collective_id=0, has_side_effects=True),
-    )(initial, coarse_guess[0], react_rate)
-    return corrected[None], defect[None]
+        compiler_params=pltpu.CompilerParams(collective_id=0, has_side_effects=True, vmem_limit_bytes=VMEM_BYTES),
+    )(*(pltpu.with_memory_space_constraint(ref, pltpu.HBM) for ref in (initial, coarse_guess[0], react_rate)))
+    return settle(corrected, defect)
 
 
 def takes_quarters(nt, planes, across):

time: 46.7 us -> 43.1 us (0.923)
  local copies, waits for them, and re-layouts: 2.8 us -> 0 us
  Pallas kernels: 43.1 us -> 42.3 us
    unnamed x4 -> x0, local copies, waits for them, and re-layouts: 2.8 us -> none
    pallas_call x1, Pallas kernels: 43.1 us -> 41.3 us  [quarter_device(): pl.pallas_call(functools.partial(quarter_kernel, nt, ns, planes, part, wi...]
    pallas_call x0 -> x1, Pallas kernels: none -> 1.03 us  [settle(): pl.pallas_call(settle_kernel, out_shape=(shape, shape), in_specs=[pl.Bloc...]
where the time goes in v2:
time: 43.1 us; the launch traced here: 42.9 us
  Pallas kernels  42.3 us (98%)
  between operations  0.64 us (1%)
    pallas_call x1, Pallas kernels, quarter_device(): pl.pallas_call(functools.partial(quarter_kernel, nt, ns, planes, part, wi...  41.3 us
    pallas_call x1, Pallas kernels, settle(): pl.pallas_call(settle_kernel, out_shape=(shape, shape), in_specs=[pl.Bloc...  1.03 us

profile of v2, /device:TPU:13, one launch (start us, length us, event | category | flops | bytes accessed | tf_op | source)
XLA Modules:
  0.0 42.9 jit_solution(2699489474851955868)
XLA Ops:
  0.6 41.3 %shard_map.50 = (f32[3,192,256]{2,1,0:T(8,128)S(1)}, f32[3,192,256]{2,1,0:T(8,128)S(1)}) custom-call(f32[3,192,256]{2,1,0:T(8,128)} %initial.1, f32[3,192,256]{2,1,0:T(8,128)} %bitcast.1, f32[3,192,256]{2,1,0:T(8,128)} %rate_in.1), custom_call_target="tpu_custom_call" | custom-call | tf_op jit(solution)/shard_map/pallas_call | solution.py:959
  41.9 1.0 %shard_map.51 = (f32[1,3,192,256]{3,2,1,0:T(8,128)}, f32[1,3,192,256]{3,2,1,0:T(8,128)}) custom-call(f32[3,192,256]{2,1,0:T(8,128)S(1)} %get-tuple-element.4.corrected, f32[3,192,256]{2,1,0:T(8,128)S(1)} %get-tuple-element.5.defect), custom_call_target="tpu_custom_call" | custom-call | tf_op jit(solution)/shard_map/pallas_call | solution.py:937

commit v3 on v2

--- a/solution.py
+++ b/solution.py
@@ -17,7 +17,8 @@
 MESH = pl.DeviceIdType.MESH
 
 PIECES = 4
-SHARES = 4
+LANES = 128
+ROW_SHARES = 2
 VMEM_BYTES = 40 << 20
 
 
@@ -550,10 +551,10 @@
         pl.when(jnp.logical_not(at_home(z)))(go[z].wait_send)
 
 
-def quarter_slots(nt):
+def quarter_slots(nt, shares):
     kinds = dict(
-        start=nt * SHARES, rate=SHARES, low_start=nt * SHARES, high_start=nt * SHARES,
-        low_rate=SHARES, high_rate=SHARES,
+        start=nt * shares, rate=shares, low_start=nt * shares, high_start=nt * shares,
+        low_rate=shares, high_rate=shares,
         low_again=nt, high_again=nt, low_first=1, high_first=1, low_offset=nt, high_offset=nt,
         corrected=nt, defect=nt,
     )
@@ -565,7 +566,7 @@
 
 
 def quarter_kernel(
-    nt, ns, planes, part, wide, recv_of, recv_total,
+    nt, ns, planes, part, wide, recv_of,
     initial, guess, rate_in, corrected_out, defect_out,
     start, again, rate, first, second, coarse, chain, offset, defect, end, reach,
     send, recv,
@@ -576,7 +577,9 @@
     levels, pairs = nt // 2, ns // 2
     length = planes + 2 * STEPS
     rows = part + 2 * wide
-    across, width = initial.shape[1], initial.shape[2]
+    across = initial.shape[1]
+    tiles = start.shape[2]
+    shares = ROW_SHARES * tiles
     low_own, high_own = STEPS, STEPS + planes
     slab = 2 * pair + core
     has_low, has_high = slab > 0, slab < ns - 1
@@ -594,17 +597,17 @@
     mine = pl.ds(2 * wide, part)
 
     first_row, last_row = y + x == 0, quarter == nt - 1
-    edge_zero = jnp.zeros((length, wide, width), jnp.float32)
+    edge_zero = jnp.zeros((length, tiles, wide, LANES), jnp.float32)
     plane_zero = jnp.zeros((STEPS,) + start.shape[2:], jnp.float32)
 
     def clear_rows(ref, k):
         @pl.when(first_row)
         def _():
-            ref[k, :, wide : 2 * wide] = edge_zero
+            ref[k, :, :, wide : 2 * wide] = edge_zero
 
         @pl.when(last_row)
         def _():
-            ref[k, :, 2 * wide + part : 3 * wide + part] = edge_zero
+            ref[k, :, :, 2 * wide + part : 3 * wide + part] = edge_zero
 
     def clear_planes(ref, k):
         @pl.when(jnp.logical_not(has_low))
@@ -640,12 +643,13 @@
     for k in range(nt):
         clear_rows(start, k)
         clear_planes(start, k)
+    for k in range(nt - 1):
         clear_planes(again, k)
-        clear_planes(chain, k)
     clear_rows(rate, 0)
     clear_planes(rate, 0)
-    clear_planes(first, 0)
-    clear_planes(second, 0)
+    clear_planes(chain, 1)
+    for j in range(2, nt - 1):
+        clear_planes(offset, j)
 
     pl.semaphore_wait(barrier, count)
 
@@ -673,34 +677,37 @@
         else:
             pl.when(condition)(copy.wait)
 
-    size = rows // SHARES
+    size = rows // ROW_SHARES
     own = pl.ds(low_own, planes)
     home = core == x
     away = jnp.logical_not(home)
 
     def source(ref, begin, share_at):
-        return ref.at[:, pl.ds(pl.multiple_of(begin + share_at * size, SUBLANES), size), :]
+        down, tile = divmod(share_at, tiles)
+        at = pl.multiple_of(begin + down * size, SUBLANES)
+        return ref.at[:, pl.ds(at, size), pl.ds(tile * LANES, LANES)]
 
     def place(ref, k, at, share_at, zs=own):
-        return ref.at[k, zs, pl.ds(pl.multiple_of(at + share_at * size, SUBLANES), size), :]
+        down, tile = divmod(share_at, tiles)
+        return ref.at[k, zs, tile, pl.ds(pl.multiple_of(at + down * size, SUBLANES), size), :]
 
     @pl.when(home)
     def _():
         for ref, k, src, kind in ((start, 0, initial, "start"), (rate, 0, rate_in, "rate")):
-            for share_at in range(SHARES):
+            for share_at in range(shares):
                 pltpu.make_async_copy(
                     source(src, my_begin, share_at), place(ref, k, my_at, share_at), recv.at[recv_of[kind] + share_at]
                 ).start()
 
     there_begin, there_at = window(2 * y + 1 - x)
-    for share_at in range(SHARES):
+    for share_at in range(shares):
         launch(
             source(initial, there_begin, share_at), place(start, 0, there_at, share_at),
             recv_of["start"] + share_at, {"tm": 2 * y + x, "space": space + 1 - 2 * x}, core == share_at % 2,
         )
     for to_y in range(levels):
         begin, at = window(2 * to_y + 1 - x)
-        for share_at in range(SHARES):
+        for share_at in range(shares):
             launch(
                 source(rate_in, begin, share_at), place(rate, 0, at, share_at), recv_of["rate"] + share_at,
                 {"tm": 2 * to_y + x, "space": space + 1 - 2 * x},
@@ -709,8 +716,8 @@
 
     def give_guess(turn):
         gives = jnp.logical_and(tm < nt - 1, core == turn)
-        for share_at in range(SHARES):
-            slot = recv_of["start"] + (tm + 1) * SHARES + share_at
+        for share_at in range(shares):
+            slot = recv_of["start"] + (tm + 1) * shares + share_at
             for dy in range(levels):
                 for dx in (1, 0):
                     to_y, to_x = lax.rem(y + dy, levels), lax.rem(x + dx, 2)
@@ -728,12 +735,12 @@
 
     give_guess(0)
 
-    row = lax.broadcasted_iota(jnp.int32, reach.shape, 0)
+    row = lax.broadcasted_iota(jnp.int32, (rows, LANES), 0)
     outside = jnp.logical_or(
         jnp.logical_and(first_row, row < wide), jnp.logical_and(last_row, row >= wide + part)
     )
-    reach[...] = jnp.where(outside, 0.0, fine_diffuse)
-    lane = lax.broadcasted_iota(jnp.int32, reach.shape, 1)
+    for zone, inside in enumerate((has_low, True, has_high)):
+        reach[zone] = jnp.where(jnp.logical_and(inside, jnp.logical_not(outside)), fine_diffuse, 0.0)
 
     def share(src_of, depth, high_slot, low_slot):
         launch(
@@ -751,59 +758,88 @@
         return lambda zs: place(start, k, my_at, share_at, zs)
 
     def relay_start(k):
-        for share_at in range(SHARES):
-            at = k * SHARES + share_at
+        for share_at in range(shares):
+            at = k * shares + share_at
             arrive(place(start, k, my_at, share_at), recv_of["start"] + at)
             share(start_view(k, share_at), STEPS, recv_of["high_start"] + at, recv_of["low_start"] + at)
 
     def start_ready(k):
-        for share_at in range(SHARES):
-            at = k * SHARES + share_at
+        for share_at in range(shares):
+            at = k * shares + share_at
             shared(start_view(k, share_at), STEPS, recv_of["high_start"] + at, recv_of["low_start"] + at)
 
     def rate_view(share_at):
         return lambda zs: place(rate, 0, my_at, share_at, zs)
 
     def relay_rate():
-        for at in range(SHARES):
+        for at in range(shares):
             arrive(place(rate, 0, my_at, at), recv_of["rate"] + at)
             share(rate_view(at), STEPS - 1, recv_of["high_rate"] + at, recv_of["low_rate"] + at)
 
     def rate_ready():
-        for at in range(SHARES):
+        for at in range(shares):
             shared(rate_view(at), STEPS - 1, recv_of["high_rate"] + at, recv_of["low_rate"] + at)
 
     def body_view(ref, k):
-        return lambda zs: ref.at[k, zs, body, :]
-
-    def change(ref, k, z):
-        middle = ref[k, z, body, :]
-        beside = ref[k, z + 1, body, :] + ref[k, z - 1, body, :]
-        beside = beside + pltpu.roll(middle, 1, 0) + pltpu.roll(middle, rows - 1, 0)
-        beside = beside + jnp.where(lane == 0, 0.0, pltpu.roll(middle, 1, 1))
-        beside = beside + jnp.where(lane == width - 1, 0.0, pltpu.roll(middle, width - 1, 1))
-        growth = rate[0, z, body, :] * (fine_growth - fine_growth * (middle * middle))
-        return middle, reach[...] * beside + middle * (growth - 6.0 * fine_diffuse)
-
-    def span(halo):
-        low = jnp.where(has_low, low_own - halo, low_own)
-        high = jnp.where(has_high, high_own + halo, high_own)
-        return low, high
-
-    def fine(src, source_k, dst, dst_k, halo, rough=False):
-        def plane(z, carry):
-            middle, delta = change(src, source_k, z)
-            dst[dst_k, z, body, :] = middle + delta
-            if rough:
-                coarse[0, z, body, :] = middle + coarse_ratio * delta
+        return lambda zs: ref.at[k, zs, :, body, :]
+
+    tall = next(number for number in (32, 16, 8) if rows % number == 0)
+    lane = lax.broadcasted_iota(jnp.int32, (tall, LANES), 1)
+
+    def march(src, k, low, high, emit):
+        def block(number, carry):
+            at = pl.multiple_of(wide + number * tall, SUBLANES)
+            here = pl.ds(at, tall)
+            reaches = [reach[zone, pl.ds(pl.multiple_of(number * tall, SUBLANES), tall), :] for zone in range(3)]
+
+            def load(z):
+                return [src[k, z, tile, here, :] for tile in range(tiles)]
+
+            under, middle = load(low - 1), load(low)
+            for z in range(low, high):
+                over = load(z + 1)
+                zone = 0 if z < low_own else 1 if z < high_own else 2
+                after = [pltpu.roll(part_of, 1, 1) for part_of in middle]
+                ahead = [pltpu.roll(part_of, LANES - 1, 1) for part_of in middle]
+                for tile in range(tiles):
+                    value = middle[tile]
+                    left = after[tile - 1] if tile else 0.0
+                    right = ahead[tile + 1] if tile + 1 < tiles else 0.0
+                    beside = over[tile] + under[tile]
+                    beside = beside + src[k, z, tile, pl.ds(at - 1, tall), :] + src[k, z, tile, pl.ds(at + 1, tall), :]
+                    beside = beside + jnp.where(lane == 0, left, after[tile])
+                    beside = beside + jnp.where(lane == LANES - 1, right, ahead[tile])
+                    growth = rate[0, z, tile, here, :] * (fine_growth - fine_growth * (value * value))
+                    stepped = reaches[zone] * beside + value * (growth + (1.0 - 6.0 * fine_diffuse))
+                    emit((z, tile, here), value, stepped)
+                under, middle = middle, over
             return carry
 
-        lax.fori_loop(*span(halo), plane, 0)
+        lax.fori_loop(0, rows // tall, block, 0)
+
+    def rough_of(value, stepped):
+        return value + coarse_ratio * (stepped - value)
+
+    def put(ref, k, spot, value):
+        z, tile, here = spot
+        ref[k, z, tile, here, :] = value
+
+    def get(ref, k, spot):
+        z, tile, here = spot
+        return ref[k, z, tile, here, :]
+
+    def fine(src, source_k, dst, halo, rough=False):
+        def emit(spot, value, stepped):
+            put(dst, 0, spot, stepped)
+            if rough and low_own <= spot[0] < high_own:
+                put(coarse, 0, spot, rough_of(value, stepped))
+
+        march(src, source_k, low_own - halo, high_own + halo, emit)
 
     def hand_in(ref, k, out, kind, j):
         there_space = 2 * pair + core
-        src = ref.at[k, own, mine, :]
-        dst = out.at[:, pl.ds(pl.multiple_of(part * quarter, SUBLANES), part), :]
+        src = ref.at[k, own, :, mine, :]
+        dst = out.at[:, :, pl.ds(pl.multiple_of(part * quarter, SUBLANES), part), :]
         slot = recv_of[kind] + quarter
         stays = jnp.logical_and(tm == j, home)
         launch(src, dst, slot, {"tm": j, "space": there_space}, jnp.logical_not(stays))
@@ -813,66 +849,58 @@
             pltpu.make_async_copy(src, dst, recv.at[slot]).start()
 
     def relax(k):
-        fine(start, k, first, 0, 2, rough=k == 0)
-        fine(first, 0, second, 0, 1)
-
-        def plane(z, carry):
-            middle, delta = change(second, 0, z)
-            value = middle + delta
+        fine(start, k, first, STEPS - 1, rough=k == 0)
+        fine(first, 0, second, STEPS - 2)
+
+        def emit(spot, value, stepped):
             if k == nt - 1:
-                defect[k, z, body, :] = end[0, z, body, :] - value
-                return carry
-            again[k, z, body, :] = value
+                put(defect, k, spot, get(end, 0, spot) - stepped)
+                return
+            put(again, k, spot, stepped)
             if k == 0:
-                defect[0, z, body, :] = value - value
-                base = coarse[0, z, body, :]
-                chain[0, z, body, :] = base + (value - base)
-            return carry
-
-        lax.fori_loop(low_own, high_own, plane, 0)
+                put(defect, 0, spot, stepped - stepped)
+                base = get(coarse, 0, spot)
+                put(chain, 0, spot, base + (stepped - base))
+
+        march(second, 0, low_own, high_own, emit)
 
     def send_again(k):
         share(body_view(again, k), STEPS, recv_of["high_again"] + k, recv_of["low_again"] + k)
 
     def finish(k):
         shared(body_view(again, k), STEPS, recv_of["high_again"] + k, recv_of["low_again"] + k)
-        fine(again, k, first, 0, 2, rough=True)
-        fine(first, 0, second, 0, 1)
-
-        def plane(z, carry):
-            middle, delta = change(second, 0, z)
-            value = middle + delta
+        fine(again, k, first, STEPS - 1, rough=True)
+        fine(first, 0, second, STEPS - 2)
+
+        def emit(spot, value, stepped):
             if k + 1 < nt - 1:
-                defect[k + 1, z, body, :] = value - again[k + 1, z, body, :]
+                put(defect, k + 1, spot, stepped - get(again, k + 1, spot))
             else:
-                end[0, z, body, :] = value
-            base = coarse[0, z, body, :]
+                put(end, 0, spot, stepped)
+            base = get(coarse, 0, spot)
             if k:
-                offset[k + 1, z, body, :] = value - base
+                put(offset, k + 1, spot, stepped - base)
             else:
-                chain[1, z, body, :] = base + (value - base)
-            return carry
-
-        lax.fori_loop(low_own, high_own, plane, 0)
+                put(chain, 1, spot, base + (stepped - base))
+
+        march(second, 0, low_own, high_own, emit)
 
     def lift_between(j, low, high):
-        def plane(z, carry):
-            middle, delta = change(chain, j - 1, z)
-            chain[j, z, body, :] = middle + coarse_ratio * delta + offset[j, z, body, :]
-            return carry
-
-        lax.fori_loop(low, high, plane, 0)
+        def emit(spot, value, stepped):
+            put(chain, j, spot, rough_of(value, stepped) + get(offset, j, spot))
+
+        march(chain, j - 1, low, high, emit)
 
     def edges_of(j):
         slots = recv_of["high_offset"] + j, recv_of["low_offset"] + j
         return body_view(offset, j), nt - 1 - j, *slots
 
     def lift_around(j):
-        if nt - 1 - j:
+        halo = nt - 1 - j
+        if halo:
             shared(*edges_of(j))
-            low, high = span(nt - 1 - j)
-            lift_between(j, low, low_own)
-            lift_between(j, high_own, high)
+            lift_between(j, low_own - halo, low_own)
+            lift_between(j, high_own, high_own + halo)
 
     relay_start(0)
     relay_rate()
@@ -898,12 +926,11 @@
             start_ready(j)
             relax(j)
             send_again(j)
-        if j + 1 < nt:
-            relay_start(j + 1)
         finish(j - 1)
         if j < nt - 1:
+            share(*edges_of(j))
+            relay_start(j + 1)
             hand_in(defect, j, defect_out, "defect", j)
-            share(*edges_of(j))
         if j == 2:
             shared(*first_edges)
         else:
@@ -918,14 +945,15 @@
         pl.when(condition)(copy.wait_send)
     for out, kind in ((corrected_out, "corrected"), (defect_out, "defect")):
         for q in range(nt):
-            arrive(out.at[:, pl.ds(part * q, part), :], recv_of[kind] + q)
+            arrive(out.at[:, :, pl.ds(part * q, part), :], recv_of[kind] + q)
 
 
 def settle_kernel(corrected, defect, corrected_out, defect_out, local):
-    copies = (
-        pltpu.make_async_copy(corrected, corrected_out.at[0], local.at[0]),
-        pltpu.make_async_copy(defect, defect_out.at[0], local.at[1]),
-    )
+    copies = []
+    for src, dst in ((corrected, corrected_out), (defect, defect_out)):
+        for tile in range(src.shape[1]):
+            to = dst.at[0, :, :, pl.ds(tile * LANES, LANES)]
+            copies.append(pltpu.make_async_copy(src.at[:, tile], to, local.at[len(copies)]))
     for copy in copies:
         copy.start()
     for copy in copies:
@@ -933,13 +961,14 @@
 
 
 def settle(corrected, defect):
-    shape = jax.ShapeDtypeStruct((1,) + corrected.shape, jnp.float32)
+    planes, tiles, across, lanes = corrected.shape
+    shape = jax.ShapeDtypeStruct((1, planes, across, tiles * lanes), jnp.float32)
     return pl.pallas_call(
         settle_kernel,
         out_shape=(shape, shape),
         in_specs=[pl.BlockSpec(memory_space=pl.ANY)] * 2,
         out_specs=[pl.BlockSpec(memory_space=pl.ANY)] * 2,
-        scratch_shapes=[pltpu.SemaphoreType.DMA((2,))],
+        scratch_shapes=[pltpu.SemaphoreType.DMA((2 * tiles,))],
         compiler_params=pltpu.CompilerParams(vmem_limit_bytes=1 << 20),
     )(corrected, defect)
 
@@ -950,21 +979,23 @@
     wide = -(-(2 * STEPS + max(nt - 2, 0)) // SUBLANES) * SUBLANES
     length = planes + 2 * STEPS
     tall = part + 4 * wide
-    recv_of, recv_total = quarter_slots(nt)
+    tiles = width // LANES
+    shares = ROW_SHARES * tiles
+    recv_of, recv_total = quarter_slots(nt, shares)
 
     def field(number):
-        return pltpu.VMEM((number, length, tall, width), jnp.float32)
-
-    shape = jax.ShapeDtypeStruct(initial.shape, jnp.float32)
+        return pltpu.VMEM((number, length, tiles, tall, LANES), jnp.float32)
+
+    shape = jax.ShapeDtypeStruct((planes, tiles, across, LANES), jnp.float32)
     corrected, defect = pl.pallas_call(
-        functools.partial(quarter_kernel, nt, ns, planes, part, wide, recv_of, recv_total),
+        functools.partial(quarter_kernel, nt, ns, planes, part, wide, recv_of),
         out_shape=(shape, shape),
         in_specs=[pl.BlockSpec(memory_space=pltpu.HBM)] * 3,
         out_specs=[pl.BlockSpec(memory_space=pl.ANY)] * 2,
         scratch_shapes=[
             field(nt), field(nt), field(1), field(1), field(1), field(1), field(nt), field(nt), field(nt), field(1),
-            pltpu.VMEM((part + 2 * wide, width), jnp.float32),
-            pltpu.SemaphoreType.DMA((SHARES * (4 * nt + nt // 2 + 3) + 6 * nt - 6,)),
+            pltpu.VMEM((3, part + 2 * wide, LANES), jnp.float32),
+            pltpu.SemaphoreType.DMA((shares * (4 * nt + nt // 2 + 3) + 6 * nt - 6,)),
             pltpu.SemaphoreType.DMA((recv_total,)),
         ],
         compiler_params=pltpu.CompilerParams(collective_id=0, has_side_effects=True, vmem_limit_bytes=VMEM_BYTES),
@@ -972,16 +1003,16 @@
     return settle(corrected, defect)
 
 
-def takes_quarters(nt, planes, across):
+def takes_quarters(nt, planes, across, width):
     part = across // nt
     wide = -(-(2 * STEPS + max(nt - 2, 0)) // SUBLANES) * SUBLANES
     fits = across % (nt * SUBLANES) == 0 and part + 2 * wide <= across and nt - 2 <= planes
-    return nt % 2 == 0 and nt > 2 and planes >= STEPS and fits
+    return nt % 2 == 0 and nt > 2 and planes >= STEPS and width % LANES == 0 and fits
 
 
 def on_device(nt, ns, initial, coarse_guess, react_rate):
     planes, across, width = initial.shape
-    if takes_quarters(nt, planes, across):
+    if takes_quarters(nt, planes, across, width):
         return quarter_device(nt, ns, initial, coarse_guess, react_rate)
     half = across // 2
     wide = -(-(2 * STEPS + max(nt - 2, 0)) // SUBLANES) * SUBLANES

time: 43.1 us -> 41.7 us (0.968)
  Pallas kernels: 42.3 us -> 40.9 us
    pallas_call x1, Pallas kernels: 41.3 us -> 39.8 us  [quarter_device(): pl.pallas_call(functools.partial(quarter_kernel, nt, ns, planes, part, wi...]
where the time goes in v3:
time: 41.7 us; the launch traced here: 41.5 us
  Pallas kernels  40.9 us (98%)
  between operations  0.64 us (2%)
    pallas_call x1, Pallas kernels, quarter_device(): pl.pallas_call(functools.partial(quarter_kernel, nt, ns, planes, part, wi...  39.8 us
    pallas_call x1, Pallas kernels, settle(): pl.pallas_call(settle_kernel, out_shape=(shape, shape), in_specs=[pl.Bloc...  1.04 us

profile of v3, /device:TPU:13, one launch (start us, length us, event | category | flops | bytes accessed | tf_op | source)
XLA Modules:
  0.0 41.5 jit_solution(14302070777233835077)
XLA Ops:
  0.6 39.8 %shard_map.50 = (f32[3,2,192,128]{3,2,1,0:T(8,128)S(1)}, f32[3,2,192,128]{3,2,1,0:T(8,128)S(1)}) custom-call(f32[3,192,256]{2,1,0:T(8,128)} %initial.1, f32[3,192,256]{2,1,0:T(8,128)} %bitcast.1, f32[3,192,256]{2,1,0:T(8,128)} %rate_in.1), custom_call_target="tpu_custom_call" | custom-call | tf_op jit(solution)/shard_map/pallas_call | solution.py:990
  40.5 1.0 %shard_map.51 = (f32[1,3,192,256]{3,2,1,0:T(8,128)}, f32[1,3,192,256]{3,2,1,0:T(8,128)}) custom-call(f32[3,2,192,128]{3,2,1,0:T(8,128)S(1)} %get-tuple-element.4.corrected, f32[3,2,192,128]{3,2,1,0:T(8,128)S(1)} %get-tuple-element.5.defect), custom_call_target="tpu_custom_call" | custom-call | tf_op jit(solution)/shard_map/pallas_call | solution.py:966

commit v4 on v3

--- a/solution.py
+++ b/solution.py
@@ -566,9 +566,9 @@
 
 
 def quarter_kernel(
-    nt, ns, planes, part, wide, recv_of,
+    nt, ns, planes, inner, wide, recv_of,
     initial, guess, rate_in, corrected_out, defect_out,
-    start, again, rate, first, second, coarse, chain, offset, defect, end, reach,
+    start, again, rate, first, second, coarse, chain, offset, defect, end,
     send, recv,
 ):
     tm, space = lax.axis_index("tm"), lax.axis_index("space")
@@ -576,38 +576,41 @@
     pair, x = lax.div(space, 2), lax.rem(space, 2)
     levels, pairs = nt // 2, ns // 2
     length = planes + 2 * STEPS
-    rows = part + 2 * wide
+    outer, most = inner + 2 * wide, inner + 3 * wide
+    less = most - wide
     across = initial.shape[1]
     tiles = start.shape[2]
     shares = ROW_SHARES * tiles
     low_own, high_own = STEPS, STEPS + planes
     slab = 2 * pair + core
     has_low, has_high = slab > 0, slab < ns - 1
-    quarter = 2 * y + x
+    edge = y == levels - 1
+    inside = jnp.logical_not(edge)
+    first_row, last_row = jnp.logical_and(edge, x == 0), jnp.logical_and(edge, x == 1)
     low_to = {"tm": tm + 1 - 2 * core, "space": space - 2 * (1 - core)}
     high_to = {"tm": tm + 1 - 2 * core, "space": space + 2 * core}
 
-    def window(which):
-        begin = jnp.clip(part * which - wide, 0, across - rows)
-        at = begin - part * which + 2 * wide
-        return pl.multiple_of(begin, SUBLANES), pl.multiple_of(at, SUBLANES)
-
-    my_begin, my_at = window(quarter)
-    body = pl.ds(wide, rows)
-    mine = pl.ds(2 * wide, part)
-
-    first_row, last_row = y + x == 0, quarter == nt - 1
+    def begin_of(to_y, to_x):
+        own_begin = outer + inner * (2 * to_y + to_x)
+        begin = jnp.where(to_y == levels - 1, to_x * (across - most), own_begin - wide)
+        return pl.multiple_of(begin, SUBLANES)
+
+    my_begin = begin_of(y, x)
+    my_part = jnp.where(edge, x * (nt - 1), 1 + 2 * y + x)
+    inset = pl.multiple_of(jnp.where(first_row, 0, wide), SUBLANES)
+    body = pl.ds(wide, most)
+
     edge_zero = jnp.zeros((length, tiles, wide, LANES), jnp.float32)
     plane_zero = jnp.zeros((STEPS,) + start.shape[2:], jnp.float32)
 
     def clear_rows(ref, k):
         @pl.when(first_row)
         def _():
-            ref[k, :, :, wide : 2 * wide] = edge_zero
+            ref[k, :, :, 0:wide] = edge_zero
 
         @pl.when(last_row)
         def _():
-            ref[k, :, :, 2 * wide + part : 3 * wide + part] = edge_zero
+            ref[k, :, :, wide + most : 2 * wide + most] = edge_zero
 
     def clear_planes(ref, k):
         @pl.when(jnp.logical_not(has_low))
@@ -644,8 +647,11 @@
         clear_rows(start, k)
         clear_planes(start, k)
     for k in range(nt - 1):
+        clear_rows(again, k)
         clear_planes(again, k)
-    clear_rows(rate, 0)
+        clear_rows(chain, k)
+    clear_rows(first, 0)
+    clear_rows(second, 0)
     clear_planes(rate, 0)
     clear_planes(chain, 1)
     for j in range(2, nt - 1):
@@ -656,62 +662,65 @@
     sends = []
     send_count = [0]
 
-    def remote(src, dst, slot, there, condition):
+    def launch(make, slot, there, condition, wider):
         number = send_count[0]
         send_count[0] += 1
-        copy = pltpu.make_async_remote_copy(
-            src_ref=src, dst_ref=dst, send_sem=send.at[number], recv_sem=recv.at[slot],
-            device_id=there, device_id_type=MESH,
-        )
-        sends.append((copy, condition))
-        return copy
-
-    def launch(src, dst, slot, there, condition):
-        copy = remote(src, dst, slot, there, condition)
-        pl.when(condition)(copy.start)
-
-    def arrive(dst, slot, condition=None):
-        copy = pltpu.make_async_copy(dst, dst, recv.at[slot])
-        if condition is None:
-            copy.wait()
-        else:
-            pl.when(condition)(copy.wait)
-
-    size = rows // ROW_SHARES
+        for rows, fits in ((most, wider), (less, jnp.logical_not(wider))):
+            src, dst = make(rows)
+            copy = pltpu.make_async_remote_copy(
+                src_ref=src, dst_ref=dst, send_sem=send.at[number], recv_sem=recv.at[slot],
+                device_id=there, device_id_type=MESH,
+            )
+            sends.append((copy, jnp.logical_and(condition, fits)))
+            pl.when(jnp.logical_and(condition, fits))(copy.start)
+
+    def local(make, slot, condition):
+        for rows, fits in ((most, edge), (less, inside)):
+            src, dst = make(rows)
+            pl.when(jnp.logical_and(condition, fits))(pltpu.make_async_copy(src, dst, recv.at[slot]).start)
+
+    def arrive(dst_of, slot, condition=True):
+        for rows, fits in ((most, edge), (less, inside)):
+            dst = dst_of(rows)
+            pl.when(jnp.logical_and(condition, fits))(pltpu.make_async_copy(dst, dst, recv.at[slot]).wait)
+
     own = pl.ds(low_own, planes)
     home = core == x
     away = jnp.logical_not(home)
 
-    def source(ref, begin, share_at):
+    cut = -(-most // (ROW_SHARES * SUBLANES)) * SUBLANES
+
+    def piece(rows, share_at):
         down, tile = divmod(share_at, tiles)
-        at = pl.multiple_of(begin + down * size, SUBLANES)
-        return ref.at[:, pl.ds(at, size), pl.ds(tile * LANES, LANES)]
-
-    def place(ref, k, at, share_at, zs=own):
-        down, tile = divmod(share_at, tiles)
-        return ref.at[k, zs, tile, pl.ds(pl.multiple_of(at + down * size, SUBLANES), size), :]
-
-    @pl.when(home)
-    def _():
-        for ref, k, src, kind in ((start, 0, initial, "start"), (rate, 0, rate_in, "rate")):
-            for share_at in range(shares):
-                pltpu.make_async_copy(
-                    source(src, my_begin, share_at), place(ref, k, my_at, share_at), recv.at[recv_of[kind] + share_at]
-                ).start()
-
-    there_begin, there_at = window(2 * y + 1 - x)
+        return tile, cut * down, min(cut * (down + 1), rows) - cut * down
+
+    def source(ref, begin, rows, share_at):
+        tile, at, size = piece(rows, share_at)
+        return ref.at[:, pl.ds(pl.multiple_of(begin + at, SUBLANES), size), pl.ds(tile * LANES, LANES)]
+
+    def place(ref, k, rows, share_at, zs=own):
+        tile, at, size = piece(rows, share_at)
+        return ref.at[k, zs, tile, pl.ds(wide + at, size), :]
+
+    def filling(src, begin, ref, k, share_at):
+        return lambda rows: (source(src, begin, rows, share_at), place(ref, k, rows, share_at))
+
+    for ref, src, kind in ((start, initial, "start"), (rate, rate_in, "rate")):
+        for share_at in range(shares):
+            local(filling(src, my_begin, ref, 0, share_at), recv_of[kind] + share_at, home)
+
+    there_begin = begin_of(y, 1 - x)
     for share_at in range(shares):
         launch(
-            source(initial, there_begin, share_at), place(start, 0, there_at, share_at),
-            recv_of["start"] + share_at, {"tm": 2 * y + x, "space": space + 1 - 2 * x}, core == share_at % 2,
+            filling(initial, there_begin, start, 0, share_at), recv_of["start"] + share_at,
+            {"tm": 2 * y + x, "space": space + 1 - 2 * x}, core == share_at % 2, edge,
         )
     for to_y in range(levels):
-        begin, at = window(2 * to_y + 1 - x)
         for share_at in range(shares):
             launch(
-                source(rate_in, begin, share_at), place(rate, 0, at, share_at), recv_of["rate"] + share_at,
+                filling(rate_in, begin_of(to_y, 1 - x), rate, 0, share_at), recv_of["rate"] + share_at,
                 {"tm": 2 * to_y + x, "space": space + 1 - 2 * x},
-                jnp.logical_and(y == levels - 1, core == share_at % 2),
+                jnp.logical_and(y == levels - 1, core == share_at % 2), jnp.bool_(to_y == levels - 1),
             )
 
     def give_guess(turn):
@@ -721,46 +730,40 @@
             for dy in range(levels):
                 for dx in (1, 0):
                     to_y, to_x = lax.rem(y + dy, levels), lax.rem(x + dx, 2)
-                    begin, at = window(2 * to_y + to_x)
-                    src, dst = source(guess, begin, share_at), place(start, tm + 1, at, share_at)
+                    make = filling(guess, begin_of(to_y, to_x), start, tm + 1, share_at)
                     there = {"tm": 2 * to_y + x, "space": 2 * pair + to_x}
                     if dy or dx:
-                        launch(src, dst, slot, there, gives)
+                        launch(make, slot, there, gives, to_y == levels - 1)
                     else:
-                        launch(src, dst, slot, there, jnp.logical_and(gives, away))
-
-                        @pl.when(jnp.logical_and(gives, home))
-                        def _(src=src, dst=dst, slot=slot):
-                            pltpu.make_async_copy(src, dst, recv.at[slot]).start()
+                        launch(make, slot, there, jnp.logical_and(gives, away), edge)
+                        local(make, slot, jnp.logical_and(gives, home))
 
     give_guess(0)
 
-    row = lax.broadcasted_iota(jnp.int32, (rows, LANES), 0)
-    outside = jnp.logical_or(
-        jnp.logical_and(first_row, row < wide), jnp.logical_and(last_row, row >= wide + part)
-    )
-    for zone, inside in enumerate((has_low, True, has_high)):
-        reach[zone] = jnp.where(jnp.logical_and(inside, jnp.logical_not(outside)), fine_diffuse, 0.0)
-
-    def share(src_of, depth, high_slot, low_slot):
-        launch(
-            src_of(pl.ds(low_own, depth)), src_of(pl.ds(high_own, depth)), high_slot, low_to, has_low
-        )
-        launch(
-            src_of(pl.ds(high_own - depth, depth)), src_of(pl.ds(low_own - depth, depth)), low_slot, high_to, has_high
-        )
-
-    def shared(dst_of, depth, high_slot, low_slot):
-        arrive(dst_of(pl.ds(high_own, depth)), high_slot, has_high)
-        arrive(dst_of(pl.ds(low_own - depth, depth)), low_slot, has_low)
+    reaches = [jnp.where(inside_of, fine_diffuse, 0.0) for inside_of in (has_low, True, has_high)]
+    reaches[1] = fine_diffuse
+
+    def share(view, depth, high_slot, low_slot):
+        def low(rows):
+            return view(pl.ds(low_own, depth), rows), view(pl.ds(high_own, depth), rows)
+
+        def high(rows):
+            return view(pl.ds(high_own - depth, depth), rows), view(pl.ds(low_own - depth, depth), rows)
+
+        launch(low, high_slot, low_to, has_low, edge)
+        launch(high, low_slot, high_to, has_high, edge)
+
+    def shared(view, depth, high_slot, low_slot):
+        arrive(lambda rows: view(pl.ds(high_own, depth), rows), high_slot, has_high)
+        arrive(lambda rows: view(pl.ds(low_own - depth, depth), rows), low_slot, has_low)
 
     def start_view(k, share_at):
-        return lambda zs: place(start, k, my_at, share_at, zs)
+        return lambda zs, rows: place(start, k, rows, share_at, zs)
 
     def relay_start(k):
         for share_at in range(shares):
             at = k * shares + share_at
-            arrive(place(start, k, my_at, share_at), recv_of["start"] + at)
+            arrive(lambda rows: place(start, k, rows, share_at), recv_of["start"] + at)
             share(start_view(k, share_at), STEPS, recv_of["high_start"] + at, recv_of["low_start"] + at)
 
     def start_ready(k):
@@ -769,11 +772,11 @@
             shared(start_view(k, share_at), STEPS, recv_of["high_start"] + at, recv_of["low_start"] + at)
 
     def rate_view(share_at):
-        return lambda zs: place(rate, 0, my_at, share_at, zs)
+        return lambda zs, rows: place(rate, 0, rows, share_at, zs)
 
     def relay_rate():
         for at in range(shares):
-            arrive(place(rate, 0, my_at, at), recv_of["rate"] + at)
+            arrive(lambda rows: place(rate, 0, rows, at), recv_of["rate"] + at)
             share(rate_view(at), STEPS - 1, recv_of["high_rate"] + at, recv_of["low_rate"] + at)
 
     def rate_ready():
@@ -781,16 +784,15 @@
             shared(rate_view(at), STEPS - 1, recv_of["high_rate"] + at, recv_of["low_rate"] + at)
 
     def body_view(ref, k):
-        return lambda zs: ref.at[k, zs, :, body, :]
-
-    tall = next(number for number in (32, 16, 8) if rows % number == 0)
+        return lambda zs, rows: ref.at[k, zs, :, pl.ds(wide, rows), :]
+
+    tall = next(number for number in (32, 16, 8) if most % number == 0)
     lane = lax.broadcasted_iota(jnp.int32, (tall, LANES), 1)
 
     def march(src, k, low, high, emit):
         def block(number, carry):
             at = pl.multiple_of(wide + number * tall, SUBLANES)
             here = pl.ds(at, tall)
-            reaches = [reach[zone, pl.ds(pl.multiple_of(number * tall, SUBLANES), tall), :] for zone in range(3)]
 
             def load(z):
                 return [src[k, z, tile, here, :] for tile in range(tiles)]
@@ -815,7 +817,7 @@
                 under, middle = middle, over
             return carry
 
-        lax.fori_loop(0, rows // tall, block, 0)
+        lax.fori_loop(0, most // tall, block, 0)
 
     def rough_of(value, stepped):
         return value + coarse_ratio * (stepped - value)
@@ -836,17 +838,21 @@
 
         march(src, source_k, low_own - halo, high_own + halo, emit)
 
+    def own_begin(number):
+        return outer + inner * (number - 1) if number else 0
+
     def hand_in(ref, k, out, kind, j):
-        there_space = 2 * pair + core
-        src = ref.at[k, own, :, mine, :]
-        dst = out.at[:, :, pl.ds(pl.multiple_of(part * quarter, SUBLANES), part), :]
-        slot = recv_of[kind] + quarter
+        begin = pl.multiple_of(my_begin + inset, SUBLANES)
+        slot = recv_of[kind] + my_part
+
+        def make(rows):
+            size = outer if rows == most else inner
+            src = ref.at[k, own, :, pl.ds(pl.multiple_of(wide + inset, SUBLANES), size), :]
+            return src, out.at[:, :, pl.ds(begin, size), :]
+
         stays = jnp.logical_and(tm == j, home)
-        launch(src, dst, slot, {"tm": j, "space": there_space}, jnp.logical_not(stays))
-
-        @pl.when(stays)
-        def _():
-            pltpu.make_async_copy(src, dst, recv.at[slot]).start()
+        launch(make, slot, {"tm": j, "space": 2 * pair + core}, jnp.logical_not(stays), edge)
+        local(make, slot, stays)
 
     def relax(k):
         fine(start, k, first, STEPS - 1, rough=k == 0)
@@ -944,8 +950,10 @@
     for copy, condition in sends:
         pl.when(condition)(copy.wait_send)
     for out, kind in ((corrected_out, "corrected"), (defect_out, "defect")):
-        for q in range(nt):
-            arrive(out.at[:, :, pl.ds(part * q, part), :], recv_of[kind] + q)
+        for number in range(nt):
+            size = inner if 0 < number < nt - 1 else outer
+            dst = out.at[:, :, pl.ds(own_begin(number), size), :]
+            pltpu.make_async_copy(dst, dst, recv.at[recv_of[kind] + number]).wait()
 
 
 def settle_kernel(corrected, defect, corrected_out, defect_out, local):
@@ -975,10 +983,9 @@
 
 def quarter_device(nt, ns, initial, coarse_guess, react_rate):
     planes, across, width = initial.shape
-    part = across // nt
-    wide = -(-(2 * STEPS + max(nt - 2, 0)) // SUBLANES) * SUBLANES
+    wide, inner = quarter_rows(nt, across)
     length = planes + 2 * STEPS
-    tall = part + 4 * wide
+    tall = inner + 5 * wide
     tiles = width // LANES
     shares = ROW_SHARES * tiles
     recv_of, recv_total = quarter_slots(nt, shares)
@@ -988,13 +995,12 @@
 
     shape = jax.ShapeDtypeStruct((planes, tiles, across, LANES), jnp.float32)
     corrected, defect = pl.pallas_call(
-        functools.partial(quarter_kernel, nt, ns, planes, part, wide, recv_of),
+        functools.partial(quarter_kernel, nt, ns, planes, inner, wide, recv_of),
         out_shape=(shape, shape),
         in_specs=[pl.BlockSpec(memory_space=pltpu.HBM)] * 3,
         out_specs=[pl.BlockSpec(memory_space=pl.ANY)] * 2,
         scratch_shapes=[
             field(nt), field(nt), field(1), field(1), field(1), field(1), field(nt), field(nt), field(nt), field(1),
-            pltpu.VMEM((3, part + 2 * wide, LANES), jnp.float32),
             pltpu.SemaphoreType.DMA((shares * (4 * nt + nt // 2 + 3) + 6 * nt - 6,)),
             pltpu.SemaphoreType.DMA((recv_total,)),
         ],
@@ -1003,10 +1009,14 @@
     return settle(corrected, defect)
 
 
+def quarter_rows(nt, across):
+    wide = -(-(2 * STEPS + max(nt - 2, 0)) // SUBLANES) * SUBLANES
+    return wide, (across - 4 * wide) // nt
+
+
 def takes_quarters(nt, planes, across, width):
-    part = across // nt
-    wide = -(-(2 * STEPS + max(nt - 2, 0)) // SUBLANES) * SUBLANES
-    fits = across % (nt * SUBLANES) == 0 and part + 2 * wide <= across and nt - 2 <= planes
+    wide, inner = quarter_rows(nt, across)
+    fits = inner > 0 and (across - 4 * wide) % (nt * SUBLANES) == 0 and nt - 2 <= planes
     return nt % 2 == 0 and nt > 2 and planes >= STEPS and width % LANES == 0 and fits
 
 

time: 41.7 us -> 38.5 us (0.923)
  Pallas kernels: 40.9 us -> 37.6 us
    pallas_call x1, Pallas kernels: 39.8 us -> 36.6 us  [quarter_device(): pl.pallas_call(functools.partial(quarter_kernel, nt, ns, planes, inner, w...]
where the time goes in v4:
time: 38.5 us; the launch traced here: 38.3 us
  Pallas kernels  37.6 us (98%)
  between operations  0.64 us (2%)
    pallas_call x1, Pallas kernels, quarter_device(): pl.pallas_call(functools.partial(quarter_kernel, nt, ns, planes, inner, w...  36.6 us
    pallas_call x1, Pallas kernels, settle(): pl.pallas_call(settle_kernel, out_shape=(shape, shape), in_specs=[pl.Bloc...  1.04 us

profile of v4, /device:TPU:13, one launch (start us, length us, event | category | flops | bytes accessed | tf_op | source)
XLA Modules:
  0.0 38.3 jit_solution(10370979301302130334)
XLA Ops:
  0.6 36.6 %shard_map.50 = (f32[3,2,192,128]{3,2,1,0:T(8,128)S(1)}, f32[3,2,192,128]{3,2,1,0:T(8,128)S(1)}) custom-call(f32[3,192,256]{2,1,0:T(8,128)} %initial.1, f32[3,192,256]{2,1,0:T(8,128)} %bitcast.1, f32[3,192,256]{2,1,0:T(8,128)} %rate_in.1), custom_call_target="tpu_custom_call" | custom-call | tf_op jit(solution)/shard_map/pallas_call | solution.py:997
  37.2 1.0 %shard_map.51 = (f32[1,3,192,256]{3,2,1,0:T(8,128)}, f32[1,3,192,256]{3,2,1,0:T(8,128)}) custom-call(f32[3,2,192,128]{3,2,1,0:T(8,128)S(1)} %get-tuple-element.4.corrected, f32[3,2,192,128]{3,2,1,0:T(8,128)S(1)} %get-tuple-element.5.defect), custom_call_target="tpu_custom_call" | custom-call | tf_op jit(solution)/shard_map/pallas_call | solution.py:974

commit v5 on v4

--- a/solution.py
+++ b/solution.py
@@ -18,7 +18,7 @@
 
 PIECES = 4
 LANES = 128
-ROW_SHARES = 2
+ROW_SHARES = 1
 VMEM_BYTES = 40 << 20
 
 

time: 38.5 us -> 37.7 us (0.979)
  Pallas kernels: 37.6 us -> 36.9 us
    pallas_call x1, Pallas kernels: 36.6 us -> 35.9 us  [quarter_device(): pl.pallas_call(functools.partial(quarter_kernel, nt, ns, planes, inner, w...]
where the time goes in v5:
time: 37.7 us; the launch traced here: 37.5 us
  Pallas kernels  36.9 us (98%)
  between operations  0.64 us (2%)
    pallas_call x1, Pallas kernels, quarter_device(): pl.pallas_call(functools.partial(quarter_kernel, nt, ns, planes, inner, w...  35.9 us
    pallas_call x1, Pallas kernels, settle(): pl.pallas_call(settle_kernel, out_shape=(shape, shape), in_specs=[pl.Bloc...  1.04 us

profile of v5, /device:TPU:13, one launch (start us, length us, event | category | flops | bytes accessed | tf_op | source)
XLA Modules:
  0.0 37.5 jit_solution(17884633173113605934)
XLA Ops:
  0.6 35.9 %shard_map.50 = (f32[3,2,192,128]{3,2,1,0:T(8,128)S(1)}, f32[3,2,192,128]{3,2,1,0:T(8,128)S(1)}) custom-call(f32[3,192,256]{2,1,0:T(8,128)} %initial.1, f32[3,192,256]{2,1,0:T(8,128)} %bitcast.1, f32[3,192,256]{2,1,0:T(8,128)} %rate_in.1), custom_call_target="tpu_custom_call" | custom-call | tf_op jit(solution)/shard_map/pallas_call | solution.py:997
  36.5 1.0 %shard_map.51 = (f32[1,3,192,256]{3,2,1,0:T(8,128)}, f32[1,3,192,256]{3,2,1,0:T(8,128)}) custom-call(f32[3,2,192,128]{3,2,1,0:T(8,128)S(1)} %get-tuple-element.4.corrected, f32[3,2,192,128]{3,2,1,0:T(8,128)S(1)} %get-tuple-element.5.defect), custom_call_target="tpu_custom_call" | custom-call | tf_op jit(solution)/shard_map/pallas_call | solution.py:974

commit v6 on v5

--- a/solution.py
+++ b/solution.py
@@ -18,7 +18,7 @@
 
 PIECES = 4
 LANES = 128
-ROW_SHARES = 1
+CORES = 2
 VMEM_BYTES = 40 << 20
 
 
@@ -551,12 +551,11 @@
         pl.when(jnp.logical_not(at_home(z)))(go[z].wait_send)
 
 
-def quarter_slots(nt, shares):
+def quarter_slots(nt, tiles):
     kinds = dict(
-        start=nt * shares, rate=shares, low_start=nt * shares, high_start=nt * shares,
-        low_rate=shares, high_rate=shares,
-        low_again=nt, high_again=nt, low_first=1, high_first=1, low_offset=nt, high_offset=nt,
-        corrected=nt, defect=nt,
+        initial=CORES * tiles, rate=CORES * tiles, guess=nt * tiles, low_start=nt * tiles, high_start=nt * tiles,
+        low_rate=tiles, high_rate=tiles, low_again=nt, high_again=nt, low_first=1, high_first=1,
+        low_offset=nt, high_offset=nt, corrected=nt, defect=nt,
     )
     first, total = {}, 0
     for kind, number in kinds.items():
@@ -580,7 +579,6 @@
     less = most - wide
     across = initial.shape[1]
     tiles = start.shape[2]
-    shares = ROW_SHARES * tiles
     low_own, high_own = STEPS, STEPS + planes
     slab = 2 * pair + core
     has_low, has_high = slab > 0, slab < ns - 1
@@ -688,49 +686,45 @@
     home = core == x
     away = jnp.logical_not(home)
 
-    cut = -(-most // (ROW_SHARES * SUBLANES)) * SUBLANES
-
-    def piece(rows, share_at):
-        down, tile = divmod(share_at, tiles)
-        return tile, cut * down, min(cut * (down + 1), rows) - cut * down
-
-    def source(ref, begin, rows, share_at):
-        tile, at, size = piece(rows, share_at)
-        return ref.at[:, pl.ds(pl.multiple_of(begin + at, SUBLANES), size), pl.ds(tile * LANES, LANES)]
-
-    def place(ref, k, rows, share_at, zs=own):
-        tile, at, size = piece(rows, share_at)
-        return ref.at[k, zs, tile, pl.ds(wide + at, size), :]
-
-    def filling(src, begin, ref, k, share_at):
-        return lambda rows: (source(src, begin, rows, share_at), place(ref, k, rows, share_at))
-
-    for ref, src, kind in ((start, initial, "start"), (rate, rate_in, "rate")):
-        for share_at in range(shares):
-            local(filling(src, my_begin, ref, 0, share_at), recv_of[kind] + share_at, home)
-
-    there_begin = begin_of(y, 1 - x)
-    for share_at in range(shares):
-        launch(
-            filling(initial, there_begin, start, 0, share_at), recv_of["start"] + share_at,
-            {"tm": 2 * y + x, "space": space + 1 - 2 * x}, core == share_at % 2, edge,
-        )
+    cut = -(-most // (CORES * SUBLANES)) * SUBLANES
+
+    def filling(src, begin, ref, k, tile, turn=None):
+        def make(rows):
+            at, size = (0, rows) if turn is None else (cut * turn, min(cut * (turn + 1), rows) - cut * turn)
+            from_rows = pl.ds(pl.multiple_of(begin + at, SUBLANES), size)
+            return src.at[:, from_rows, pl.ds(tile * LANES, LANES)], ref.at[k, own, tile, pl.ds(wide + at, size), :]
+
+        return make
+
+    def arrive_filling(ref, k, tile, slot, turn=None):
+        arrive(lambda rows: filling(initial, 0, ref, k, tile, turn)(rows)[1], slot)
+
+    for ref, src, kind in ((start, initial, "initial"), (rate, rate_in, "rate")):
+        for tile in range(tiles):
+            for turn in range(CORES):
+                local(filling(src, my_begin, ref, 0, tile, turn), recv_of[kind] + CORES * tile + turn, home)
+
+    def give_split(src, ref, kind, to_y, condition, wider):
+        begin = begin_of(to_y, 1 - x)
+        for tile in range(tiles):
+            for turn in range(CORES):
+                launch(
+                    filling(src, begin, ref, 0, tile, turn), recv_of[kind] + CORES * tile + turn,
+                    {"tm": 2 * to_y + x, "space": space + 1 - 2 * x}, jnp.logical_and(condition, core == turn), wider,
+                )
+
+    give_split(initial, start, "initial", y, jnp.bool_(True), edge)
     for to_y in range(levels):
-        for share_at in range(shares):
-            launch(
-                filling(rate_in, begin_of(to_y, 1 - x), rate, 0, share_at), recv_of["rate"] + share_at,
-                {"tm": 2 * to_y + x, "space": space + 1 - 2 * x},
-                jnp.logical_and(y == levels - 1, core == share_at % 2), jnp.bool_(to_y == levels - 1),
-            )
+        give_split(rate_in, rate, "rate", to_y, edge, jnp.bool_(to_y == levels - 1))
 
     def give_guess(turn):
         gives = jnp.logical_and(tm < nt - 1, core == turn)
-        for share_at in range(shares):
-            slot = recv_of["start"] + (tm + 1) * shares + share_at
+        for tile in range(tiles):
+            slot = recv_of["guess"] + (tm + 1) * tiles + tile
             for dy in range(levels):
                 for dx in (1, 0):
                     to_y, to_x = lax.rem(y + dy, levels), lax.rem(x + dx, 2)
-                    make = filling(guess, begin_of(to_y, to_x), start, tm + 1, share_at)
+                    make = filling(guess, begin_of(to_y, to_x), start, tm + 1, tile)
                     there = {"tm": 2 * to_y + x, "space": 2 * pair + to_x}
                     if dy or dx:
                         launch(make, slot, there, gives, to_y == levels - 1)
@@ -757,31 +751,33 @@
         arrive(lambda rows: view(pl.ds(high_own, depth), rows), high_slot, has_high)
         arrive(lambda rows: view(pl.ds(low_own - depth, depth), rows), low_slot, has_low)
 
-    def start_view(k, share_at):
-        return lambda zs, rows: place(start, k, rows, share_at, zs)
+    def tile_view(ref, k, tile):
+        return lambda zs, rows: ref.at[k, zs, tile, pl.ds(wide, rows), :]
 
     def relay_start(k):
-        for share_at in range(shares):
-            at = k * shares + share_at
-            arrive(lambda rows: place(start, k, rows, share_at), recv_of["start"] + at)
-            share(start_view(k, share_at), STEPS, recv_of["high_start"] + at, recv_of["low_start"] + at)
+        for tile in range(tiles):
+            if k:
+                arrive_filling(start, k, tile, recv_of["guess"] + k * tiles + tile)
+            else:
+                for turn in range(CORES):
+                    arrive_filling(start, 0, tile, recv_of["initial"] + CORES * tile + turn, turn)
+            at = k * tiles + tile
+            share(tile_view(start, k, tile), STEPS, recv_of["high_start"] + at, recv_of["low_start"] + at)
 
     def start_ready(k):
-        for share_at in range(shares):
-            at = k * shares + share_at
-            shared(start_view(k, share_at), STEPS, recv_of["high_start"] + at, recv_of["low_start"] + at)
-
-    def rate_view(share_at):
-        return lambda zs, rows: place(rate, 0, rows, share_at, zs)
+        for tile in range(tiles):
+            at = k * tiles + tile
+            shared(tile_view(start, k, tile), STEPS, recv_of["high_start"] + at, recv_of["low_start"] + at)
 
     def relay_rate():
-        for at in range(shares):
-            arrive(lambda rows: place(rate, 0, rows, at), recv_of["rate"] + at)
-            share(rate_view(at), STEPS - 1, recv_of["high_rate"] + at, recv_of["low_rate"] + at)
+        for tile in range(tiles):
+            for turn in range(CORES):
+                arrive_filling(rate, 0, tile, recv_of["rate"] + CORES * tile + turn, turn)
+            share(tile_view(rate, 0, tile), STEPS - 1, recv_of["high_rate"] + tile, recv_of["low_rate"] + tile)
 
     def rate_ready():
-        for at in range(shares):
-            shared(rate_view(at), STEPS - 1, recv_of["high_rate"] + at, recv_of["low_rate"] + at)
+        for tile in range(tiles):
+            shared(tile_view(rate, 0, tile), STEPS - 1, recv_of["high_rate"] + tile, recv_of["low_rate"] + tile)
 
     def body_view(ref, k):
         return lambda zs, rows: ref.at[k, zs, :, pl.ds(wide, rows), :]
@@ -987,8 +983,7 @@
     length = planes + 2 * STEPS
     tall = inner + 5 * wide
     tiles = width // LANES
-    shares = ROW_SHARES * tiles
-    recv_of, recv_total = quarter_slots(nt, shares)
+    recv_of, recv_total = quarter_slots(nt, tiles)
 
     def field(number):
         return pltpu.VMEM((number, length, tiles, tall, LANES), jnp.float32)
@@ -1001,7 +996,7 @@
         out_specs=[pl.BlockSpec(memory_space=pl.ANY)] * 2,
         scratch_shapes=[
             field(nt), field(nt), field(1), field(1), field(1), field(1), field(nt), field(nt), field(nt), field(1),
-            pltpu.SemaphoreType.DMA((shares * (4 * nt + nt // 2 + 3) + 6 * nt - 6,)),
+            pltpu.SemaphoreType.DMA((tiles * (CORES * (1 + nt // 2) + 4 * nt + 2) + 6 * nt - 6,)),
             pltpu.SemaphoreType.DMA((recv_total,)),
         ],
         compiler_params=pltpu.CompilerParams(collective_id=0, has_side_effects=True, vmem_limit_bytes=VMEM_BYTES),

time: 37.7 us -> 37.3 us (0.989)
  Pallas kernels: 36.9 us -> 36.5 us
    pallas_call x1, Pallas kernels: 35.9 us -> 35.4 us  [quarter_device(): pl.pallas_call(functools.partial(quarter_kernel, nt, ns, planes, inner, w...]
where the time goes in v6:
time: 37.3 us; the launch traced here: 37.1 us
  Pallas kernels  36.5 us (98%)
  between operations  0.64 us (2%)
    pallas_call x1, Pallas kernels, quarter_device(): pl.pallas_call(functools.partial(quarter_kernel, nt, ns, planes, inner, w...  35.4 us
    pallas_call x1, Pallas kernels, settle(): pl.pallas_call(settle_kernel, out_shape=(shape, shape), in_specs=[pl.Bloc...  1.04 us

profile of v6, /device:TPU:13, one launch (start us, length us, event | category | flops | bytes accessed | tf_op | source)
XLA Modules:
  0.0 37.1 jit_solution(15692350443719501270)
XLA Ops:
  0.6 35.4 %shard_map.50 = (f32[3,2,192,128]{3,2,1,0:T(8,128)S(1)}, f32[3,2,192,128]{3,2,1,0:T(8,128)S(1)}) custom-call(f32[3,192,256]{2,1,0:T(8,128)} %initial.1, f32[3,192,256]{2,1,0:T(8,128)} %bitcast.1, f32[3,192,256]{2,1,0:T(8,128)} %rate_in.1), custom_call_target="tpu_custom_call" | custom-call | tf_op jit(solution)/shard_map/pallas_call | solution.py:992
  36.1 1.0 %shard_map.51 = (f32[1,3,192,256]{3,2,1,0:T(8,128)}, f32[1,3,192,256]{3,2,1,0:T(8,128)}) custom-call(f32[3,2,192,128]{3,2,1,0:T(8,128)S(1)} %get-tuple-element.4.corrected, f32[3,2,192,128]{3,2,1,0:T(8,128)S(1)} %get-tuple-element.5.defect), custom_call_target="tpu_custom_call" | custom-call | tf_op jit(solution)/shard_map/pallas_call | solution.py:970

commit v7 on v6

--- a/solution.py
+++ b/solution.py
@@ -782,7 +782,7 @@
     def body_view(ref, k):
         return lambda zs, rows: ref.at[k, zs, :, pl.ds(wide, rows), :]
 
-    tall = next(number for number in (32, 16, 8) if most % number == 0)
+    tall = next(number for number in (64, 32, 16, 8) if most % number == 0)
     lane = lax.broadcasted_iota(jnp.int32, (tall, LANES), 1)
 
     def march(src, k, low, high, emit):

time: 37.3 us -> 36.7 us (0.984)
  Pallas kernels: 36.5 us -> 35.9 us
    pallas_call x1, Pallas kernels: 35.4 us -> 34.8 us  [quarter_device(): pl.pallas_call(functools.partial(quarter_kernel, nt, ns, planes, inner, w...]
where the time goes in v7:
time: 36.7 us; the launch traced here: 36.5 us
  Pallas kernels  35.9 us (98%)
  between operations  0.64 us (2%)
    pallas_call x1, Pallas kernels, quarter_device(): pl.pallas_call(functools.partial(quarter_kernel, nt, ns, planes, inner, w...  34.8 us
    pallas_call x1, Pallas kernels, settle(): pl.pallas_call(settle_kernel, out_shape=(shape, shape), in_specs=[pl.Bloc...  1.04 us

profile of v7, /device:TPU:13, one launch (start us, length us, event | category | flops | bytes accessed | tf_op | source)
XLA Modules:
  0.0 36.5 jit_solution(17716248949914440903)
XLA Ops:
  0.6 34.8 %shard_map.50 = (f32[3,2,192,128]{3,2,1,0:T(8,128)S(1)}, f32[3,2,192,128]{3,2,1,0:T(8,128)S(1)}) custom-call(f32[3,192,256]{2,1,0:T(8,128)} %initial.1, f32[3,192,256]{2,1,0:T(8,128)} %bitcast.1, f32[3,192,256]{2,1,0:T(8,128)} %rate_in.1), custom_call_target="tpu_custom_call" | custom-call | tf_op jit(solution)/shard_map/pallas_call | solution.py:992
  35.4 1.0 %shard_map.51 = (f32[1,3,192,256]{3,2,1,0:T(8,128)}, f32[1,3,192,256]{3,2,1,0:T(8,128)}) custom-call(f32[3,2,192,128]{3,2,1,0:T(8,128)S(1)} %get-tuple-element.4.corrected, f32[3,2,192,128]{3,2,1,0:T(8,128)S(1)} %get-tuple-element.5.defect), custom_call_target="tpu_custom_call" | custom-call | tf_op jit(solution)/shard_map/pallas_call | solution.py:970

commit v8 on v7

--- a/solution.py
+++ b/solution.py
@@ -719,12 +719,13 @@
 
     def give_guess(turn):
         gives = jnp.logical_and(tm < nt - 1, core == turn)
+        number = jnp.minimum(tm + 1, nt - 1)
         for tile in range(tiles):
-            slot = recv_of["guess"] + (tm + 1) * tiles + tile
+            slot = recv_of["guess"] + number * tiles + tile
             for dy in range(levels):
                 for dx in (1, 0):
                     to_y, to_x = lax.rem(y + dy, levels), lax.rem(x + dx, 2)
-                    make = filling(guess, begin_of(to_y, to_x), start, tm + 1, tile)
+                    make = filling(guess, begin_of(to_y, to_x), start, number, tile)
                     there = {"tm": 2 * to_y + x, "space": 2 * pair + to_x}
                     if dy or dx:
                         launch(make, slot, there, gives, to_y == levels - 1)

time: 36.7 us -> 36.7 us (level)
  no operation moved by 1% of the time
where the time goes in v8:
time: 36.7 us; the launch traced here: 36.5 us
  Pallas kernels  35.9 us (98%)
  between operations  0.64 us (2%)
    pallas_call x1, Pallas kernels, quarter_device(): pl.pallas_call(functools.partial(quarter_kernel, nt, ns, planes, inner, w...  34.8 us
    pallas_call x1, Pallas kernels, settle(): pl.pallas_call(settle_kernel, out_shape=(shape, shape), in_specs=[pl.Bloc...  1.04 us

profile of v8, /device:TPU:13, one launch (start us, length us, event | category | flops | bytes accessed | tf_op | source)
XLA Modules:
  0.0 36.5 jit_solution(330218570352960839)
XLA Ops:
  0.6 34.8 %shard_map.50 = (f32[3,2,192,128]{3,2,1,0:T(8,128)S(1)}, f32[3,2,192,128]{3,2,1,0:T(8,128)S(1)}) custom-call(f32[3,192,256]{2,1,0:T(8,128)} %initial.1, f32[3,192,256]{2,1,0:T(8,128)} %bitcast.1, f32[3,192,256]{2,1,0:T(8,128)} %rate_in.1), custom_call_target="tpu_custom_call" | custom-call | tf_op jit(solution)/shard_map/pallas_call | solution.py:993
  35.4 1.0 %shard_map.51 = (f32[1,3,192,256]{3,2,1,0:T(8,128)}, f32[1,3,192,256]{3,2,1,0:T(8,128)}) custom-call(f32[3,2,192,128]{3,2,1,0:T(8,128)S(1)} %get-tuple-element.4.corrected, f32[3,2,192,128]{3,2,1,0:T(8,128)S(1)} %get-tuple-element.5.defect), custom_call_target="tpu_custom_call" | custom-call | tf_op jit(solution)/shard_map/pallas_call | solution.py:971

commit v9 on v8

--- a/solution.py
+++ b/solution.py
@@ -699,11 +699,6 @@
     def arrive_filling(ref, k, tile, slot, turn=None):
         arrive(lambda rows: filling(initial, 0, ref, k, tile, turn)(rows)[1], slot)
 
-    for ref, src, kind in ((start, initial, "initial"), (rate, rate_in, "rate")):
-        for tile in range(tiles):
-            for turn in range(CORES):
-                local(filling(src, my_begin, ref, 0, tile, turn), recv_of[kind] + CORES * tile + turn, home)
-
     def give_split(src, ref, kind, to_y, condition, wider):
         begin = begin_of(to_y, 1 - x)
         for tile in range(tiles):
@@ -714,6 +709,11 @@
                 )
 
     give_split(initial, start, "initial", y, jnp.bool_(True), edge)
+    for ref, src, kind in ((start, initial, "initial"), (rate, rate_in, "rate")):
+        for tile in range(tiles):
+            for turn in range(CORES):
+                local(filling(src, my_begin, ref, 0, tile, turn), recv_of[kind] + CORES * tile + turn, home)
+
     for to_y in range(levels):
         give_split(rate_in, rate, "rate", to_y, edge, jnp.bool_(to_y == levels - 1))
 

time: 36.7 us -> 36.7 us (level)
  no operation moved by 1% of the time
where the time goes in v9:
time: 36.7 us; the launch traced here: 36.5 us
  Pallas kernels  35.9 us (98%)
  between operations  0.64 us (2%)
    pallas_call x1, Pallas kernels, quarter_device(): pl.pallas_call(functools.partial(quarter_kernel, nt, ns, planes, inner, w...  34.8 us
    pallas_call x1, Pallas kernels, settle(): pl.pallas_call(settle_kernel, out_shape=(shape, shape), in_specs=[pl.Bloc...  1.04 us

profile of v9, /device:TPU:13, one launch (start us, length us, event | category | flops | bytes accessed | tf_op | source)
XLA Modules:
  0.0 36.5 jit_solution(13848859578866033488)
XLA Ops:
  0.6 34.8 %shard_map.50 = (f32[3,2,192,128]{3,2,1,0:T(8,128)S(1)}, f32[3,2,192,128]{3,2,1,0:T(8,128)S(1)}) custom-call(f32[3,192,256]{2,1,0:T(8,128)} %initial.1, f32[3,192,256]{2,1,0:T(8,128)} %bitcast.1, f32[3,192,256]{2,1,0:T(8,128)} %rate_in.1), custom_call_target="tpu_custom_call" | custom-call | tf_op jit(solution)/shard_map/pallas_call | solution.py:993
  35.4 1.0 %shard_map.51 = (f32[1,3,192,256]{3,2,1,0:T(8,128)}, f32[1,3,192,256]{3,2,1,0:T(8,128)}) custom-call(f32[3,2,192,128]{3,2,1,0:T(8,128)S(1)} %get-tuple-element.4.corrected, f32[3,2,192,128]{3,2,1,0:T(8,128)S(1)} %get-tuple-element.5.defect), custom_call_target="tpu_custom_call" | custom-call | tf_op jit(solution)/shard_map/pallas_call | solution.py:971
